TPU v7x, 512 devices: a whole 4x4x16 slice. The times are simulated.
512 devices in a mesh: space: 128 (over x, z, core), mem: 4 (over y).
Axes of the slice: x: 4, y: 4, z: 16, core: 2. Of those that a mesh axis runs over, the one named last changes fastest.
Arguments:
- state: float32 [64, 3, 2048, 256], P('mem', None, 'space'), may hold values from -6 to 6
- depth: float32 [2048, 256], P('space'), may hold values from 0.5 to 2
- obs_cells: int32 [4, 8192, 128], P(None, 'space'), may hold values from 0 to 4095, as said below
- obs_weights: float32 [4, 8192, 128], P(None, 'space'), may hold values from 0 to 0.5
- owner_map: int32 [8192, 1], P('space'), may hold values from 0 to 127; in each aligned block of 64 rows (0 to 63, 64 to 127, ...) at most 2 rows name the same one
- obs_values: float32 [128, 128, 2, 128], P('space'), may hold values from -8 to 8
- obs_precision: float32 [128, 128, 2, 128], P('space'), may hold values from 0.5 to 6
Outputs:
- analysis: float32 [64, 3, 2048, 256], P('mem', None, 'space')
Inputs may be any that keep to these rules, and one draw needn't show every extreme that they name: The cells of block b lie in the rows of space device b // 64; obs_cells is the offset within those rows. `owner_map`: among the 64 blocks of one space device no owner is named more than 2 times, and in some device one owner is named exactly 2 times.
All inputs are finite; a program needn't handle non-finite values.
Results may differ from a plain program's by a relative error of at most 0.00012.
Values sent between devices are 32-bit elements; how exact they have to be, the bound alone decides.
A program may use at most 64 MiB of HBM per device.

v0:
```python
import math

import jax
import jax.numpy as jnp
from jax import lax
from jax.sharding import PartitionSpec as P

M = 64
STEPS = 2


mass_rate = 0.2
wave_rate = 0.2
turn_rate = 0.1


def with_halo(cells, sides, width):
    for axis, dim in sides:
        count = lax.axis_size(axis)
        ends = count - 1
        head = lax.slice_in_dim(cells, 0, width, axis=dim)
        tail = lax.slice_in_dim(cells, cells.shape[dim] - width, cells.shape[dim], axis=dim)
        cells = jnp.concatenate(
            [
                lax.ppermute(tail, axis, [(i, (i + 1) % count) for i in range(ends)]),
                cells,
                lax.ppermute(head, axis, [((i + 1) % count, i) for i in range(ends)]),
            ],
            axis=dim,
        )
    return cells


def diff_cols(field):
    return jnp.roll(field, -1, axis=-1) - jnp.roll(field, 1, axis=-1)


def gram_terms(values, seen, weight, scale):
    middle = jnp.mean(values, axis=0)
    factor = weight * scale
    scaled = (values - middle[None]) * factor[None]
    depart = (seen - middle) * factor
    gram = jnp.einsum("mrk,nrk->mn", scaled, scaled, precision=lax.Precision.HIGHEST)
    proj = jnp.einsum("mrk,rk->m", scaled, depart, precision=lax.Precision.HIGHEST)
    return (gram, proj)


def make_mixing(lower, proj, members):
    eye = jnp.eye(members, dtype=jnp.float32)
    first = lax.linalg.triangular_solve(lower, proj[:, None], left_side=True, lower=True)
    mean_weights = lax.linalg.triangular_solve(
        lower, first, left_side=True, lower=True, transpose_a=True
    )[:, 0]
    inverse_lower = lax.linalg.triangular_solve(lower, eye, left_side=True, lower=True)
    spread = math.sqrt(members - 1) * inverse_lower.T
    coef = mean_weights[:, None] + spread
    return coef + (1.0 - jnp.sum(coef, axis=0))[None, :] / members


def local(state, depth, obs_cells, obs_weights, owner_map, obs_values, obs_precision):
    local_ensemble, fields, horizontal_sums, vertical_sums = state.shape
    count = lax.axis_size("space")
    quarter = lax.axis_index("mem")
    fluid_elevation, zonal_wind, meridional_wind = (state[:, 0], state[:, 1], state[:, 2])
    for step in range(STEPS):
        flux_rimmed = with_halo(depth * zonal_wind, (("space", 1),), 1)
        fluid_elevation = fluid_elevation - mass_rate * (
            flux_rimmed[:, 2:] - flux_rimmed[:, :-2] + diff_cols(depth * meridional_wind)
        )
        height_rimmed = with_halo(fluid_elevation, (("space", 1),), 1)
        east_new = (
            zonal_wind
            - wave_rate * (height_rimmed[:, 2:] - height_rimmed[:, :-2])
            + turn_rate * meridional_wind
        )
        meridional_wind = (
            meridional_wind - wave_rate * diff_cols(fluid_elevation) - turn_rate * zonal_wind
        )
        zonal_wind = east_new
    prior_fields = jnp.stack([fluid_elevation, zonal_wind, meridional_wind], axis=1)
    src_blocks = obs_cells.shape[1]
    obs_width = obs_cells.shape[2]
    pair_cap = obs_values.shape[2]
    flat = fluid_elevation.reshape(local_ensemble, horizontal_sums * vertical_sums)
    predicted = jnp.sum(obs_weights[None] * flat[:, obs_cells], axis=1)
    owners = owner_map[:, 0]
    same = (owners[:, None] == owners[None, :]).astype(jnp.int32)
    order = jnp.arange(src_blocks, dtype=jnp.int32)
    earlier = (order[:, None] < order[None, :]).astype(jnp.int32)
    slots = jnp.sum(same * earlier, axis=0)
    scale = math.sqrt((M - 1) / (count * src_blocks * obs_width))
    target = owners * pair_cap + slots
    outgoing = (
        jnp.zeros((local_ensemble, count * pair_cap, obs_width), jnp.float32)
        .at[:, target]
        .set(predicted)
    )
    arrived = lax.all_to_all(
        lax.all_to_all(outgoing, "space", split_axis=1, concat_axis=1, tiled=True),
        "mem",
        split_axis=1,
        concat_axis=0,
        tiled=True,
    )
    share = arrived.shape[1]
    value_rows = obs_values[0].reshape(count * pair_cap, obs_width)
    weight_rows = obs_precision[0].reshape(count * pair_cap, obs_width)
    seen = lax.dynamic_slice_in_dim(value_rows, quarter * share, share, 0)
    weight = lax.dynamic_slice_in_dim(weight_rows, quarter * share, share, 0)
    gram, proj = gram_terms(arrived, seen, weight, scale)
    eye = jnp.eye(M, dtype=jnp.float32)
    gram, proj = lax.psum((gram, proj), ("space", "mem"))
    lower = jnp.linalg.cholesky((M - 1) * eye + gram)
    transform_weights = make_mixing(lower, proj, M)
    my_columns = lax.dynamic_slice_in_dim(
        transform_weights, quarter * local_ensemble, local_ensemble, 1
    )
    prior_vector = prior_fields.reshape(local_ensemble, 3 * horizontal_sums * vertical_sums)
    combined = jnp.einsum(
        "ij,ic->jc",
        my_columns,
        lax.all_gather(prior_vector, "mem", axis=0, tiled=True),
        precision=lax.Precision.HIGHEST,
    )
    return combined.reshape(local_ensemble, 3, horizontal_sums, vertical_sums)


def solution(mesh):
    return jax.shard_map(
        local,
        mesh=mesh,
        in_specs=(
            P("mem", None, "space", None),
            P("space", None),
            P(None, "space", None),
            P(None, "space", None),
            P("space", None),
            P("space", None, None, None),
            P("space", None, None, None),
        ),
        out_specs=P("mem", None, "space", None),
        check_vma=False,
    )
```

profile of v0, /device:TPU:1, one launch (start us, length us, event | category | flops | bytes accessed | tf_op | source)
XLA Modules:
  0.0 461.7 jit_solution(6934445929983753596)
XLA Ops:
  6.5 1.1 bitcast_multiply_fusion.1
  7.7 8.7 %collective-permute-start = (f32[16,1,256]{2,1,0:T(1,128)S(1)}, f32[16,1,256]{2,1,0:T(1,128)S(1)}, u32[]{:S(2)}, u32[]{:S(2)}) collective-permute-start(f32[16,1,256]{2,1,0:T(1,128)S(1)} %get-tuple-element.39), channel_id=1, source_target_pairs={{4,0},{8,4},{12,8},{16,12},{20,16},{24,20},{28,24},{32,28},{36,32}... | collective-permute-start | bytes 49160 | tf_op jit(solution)/shard_map/ppermute | solution.py:27
  16.5 1.9 collective-permute-start.1
  19.9 2.1 collective-permute-start.2
  22.0 3.7 collective-permute-start.3
  25.9 0.7 collective-permute-done.3
  27.0 1.9 collective-permute-start.4
  29.0 4.2 collective-permute-start.5
  33.3 0.7 collective-permute-done.5
  34.9 108.4 %gather_fusion = f32[32768,16]{1,0:T(8,128)} fusion(f32[16,4096]{0,1:T(8,128)S(1)} %bitcast.89, s32[32768]{0:T(1024)S(1)} %broadcast_clamp_fusion), kind=kCustom, calls=%fused_computation | custom fusion | bytes 4325376 | tf_op jit(solution)/shard_map/gather | solution.py:85
  143.2 9.8 %multiply_reduce_fusion = f32[64,128,16]{2,1,0:T(8,128)} fusion(f32[4,64,128,16]{3,2,1,0:T(8,128)} %bitcast.90, f32[4,64,128]{2,1,0:T(8,128)S(1)} %copy-done.1), kind=kLoop, calls=%fused_computation.2 | loop fusion | flops 917504 | bytes 2752512 | tf_op jit(solution)/shard_map/reduce_sum | solution.py:85
  153.0 2.8 copy.29
  155.8 1.5 broadcast_in_dim.5
  157.3 7.1 %scatter_fusion = f32[16,256,128]{2,0,1:T(8,128)} fusion(f32[16,256,128]{2,0,1:T(8,128)} %broadcast_in_dim.5, s32[64]{0:T(128)S(1)} %fusion.34, f32[64,16,128]{2,1,0:T(8,128)S(1)} %copy.29), kind=kCustom, calls=%fused_computation.1 | custom fusion | bytes 1573120 | tf_op jit(solution)/shard_map/scatter | solution.py:96
  164.4 19.9 %all-to-all-start = ((f32[16,256,128]{2,0,1:T(8,128)}), f32[16,256,128]{2,0,1:T(8,128)}, u32[]{:S(2)}, u32[]{:S(2)}) async-start(f32[16,256,128]{2,0,1:T(8,128)} %scatter_fusion), calls=%async_computation | async-start | bytes 4194304 | tf_op jit(solution)/shard_map/all_to_all | solution.py:99
  184.4 2.9 collective-permute-start.6
  187.3 2.7 collective-permute-start.7
  190.3 84.2 %collective-permute-done.6 = f32[16,1,256]{2,1,0:T(1,128)S(1)} collective-permute-done((f32[16,1,256]{2,1,0:T(1,128)S(1)}, f32[16,1,256]{2,1,0:T(1,128)S(1)}, u32[]{:S(2)}, u32[]{:S(2)}) %collective-permute-start.6) | collective-permute-done | bytes 16416 | tf_op jit(solution)/shard_map/ppermute | solution.py:27
  274.8 1.3 copy.36
  276.1 7.0 %all-to-all-done = f32[16,256,128]{2,0,1:T(8,128)} async-done(((f32[16,256,128]{2,0,1:T(8,128)}), f32[16,256,128]{2,0,1:T(8,128)}, u32[]{:S(2)}, u32[]{:S(2)}) %all-to-all-start) | async-done | bytes 2097184 | tf_op jit(solution)/shard_map/all_to_all | solution.py:99
  283.2 4.2 all-to-all-start.1
  287.4 38.6 %all-to-all-done.1 = f32[16,256,128]{2,0,1:T(8,128)S(1)} async-done(((f32[16,256,128]{2,0,1:T(8,128)}), f32[16,256,128]{2,0,1:T(8,128)S(1)}, u32[]{:S(2)}, u32[]{:S(2)}) %all-to-all-start.1) | async-done | bytes 2097184 | tf_op jit(solution)/shard_map/all_to_all | solution.py:98
  326.0 1.7 copy.30
  327.8 0.8 subtract_multiply_fusion
  328.6 2.0 fusion
  330.7 1.7 convolution_bitcast_fusion.3
  332.4 1.8 convolution_bitcast_fusion
  334.2 103.2 %all-reduce = (f32[64,64]{1,0:T(8,128)S(1)}, f32[64]{0:T(128)S(1)}) all-reduce(f32[64,64]{1,0:T(8,128)S(1)} %convolution_bitcast_fusion, f32[64]{0:T(128)S(1)} %convolution_bitcast_fusion.3), channel_id=1, replica_groups=mesh['space'=128,'mem'=4] {'space','mem'}, use_global_device_ids=true, to_apply=%region_4.5 | all-reduce | flops 4160 | bytes 33280 | tf_op jit(solution)/shard_map/psum | solution.py:112
  437.5 5.8 %cholesky.17 = f32[64,64]{1,0:T(8,128)S(1)} custom-call(f32[64,64]{1,0:T(8,128)S(1)} %fusion.30), custom_call_target="Cholesky" | custom-call | tf_op jit(solution)/shard_map/jit(cholesky)/cholesky | solution.py:113
  444.6 4.9 %custom-call.10 = f32[1,64,64]{1,2,0:T(8,128)S(1)} custom-call(f32[1,64,64]{2,1,0:T(8,128)S(1)} %fusion.26), custom_call_target="InvertDiagBlocksLowerTriangular" | custom-call | tf_op jit(solution)/shard_map/triangular_solve | solution.py:51
  450.2 3.5 fusion.31
  453.7 1.1 copy.37
  (53 shorter events, 5.8 us)
Async XLA Ops:
  6.5 13.0 %copy-start = (f32[16,3,16,256]{3,2,1,0:T(8,128)S(1)}, f32[16,3,16,256]{3,2,1,0:T(8,128)}, u32[]{:S(2)}) copy-start(f32[16,3,16,256]{3,2,1,0:T(8,128)} %param.7) | copy-start | bytes 2359300
  6.5 12.1 %copy-start.2 = (s32[4,64,128]{2,1,0:T(8,128)S(1)}, s32[4,64,128]{2,1,0:T(8,128)}, u32[]{:S(2)}) copy-start(s32[4,64,128]{2,1,0:T(8,128)} %param.9) | copy-start | bytes 393220
  6.5 12.2 %copy-start.4 = (s32[64,1]{0,1:T(1,128)S(1)}, s32[64,1]{0,1:T(1,128)}, u32[]{:S(2)}) copy-start(s32[64,1]{0,1:T(1,128)} %param.11) | copy-start | bytes 772
  7.7 11.1 %collective-permute-start = (f32[16,1,256]{2,1,0:T(1,128)S(1)}, f32[16,1,256]{2,1,0:T(1,128)S(1)}, u32[]{:S(2)}, u32[]{:S(2)}) collective-permute-start(f32[16,1,256]{2,1,0:T(1,128)S(1)} %get-tuple-element.39), channel_id=1, source_target_pairs={{4,0},{8,4},{12,8},{16,12},{20,16},{24,20},{28,24},{32,28},{36,32}... | collective-permute-start | bytes 49160 | tf_op jit(solution)/shard_map/ppermute | solution.py:27
  16.5 3.1 collective-permute-start.1
  18.6 8.1 %copy-start.3 = (f32[16,256]{1,0:T(8,128)S(1)}, f32[16,256]{1,0:T(8,128)}, u32[]{:S(2)}) copy-start(f32[16,256]{1,0:T(8,128)} %param.8) | copy-start | bytes 49156
  19.9 5.9 %collective-permute-start.2 = (f32[16,1,256]{2,1,0:T(1,128)S(1)}, f32[16,1,256]{2,1,0:T(1,128)S(1)}, u32[]{:S(2)}, u32[]{:S(2)}) collective-permute-start(f32[16,1,256]{2,1,0:T(1,128)S(1)} %get-tuple-element.29), channel_id=1, source_target_pairs={{4,0},{8,4},{12,8},{16,12},{20,16},{24,20},{28,24},{32,28},{36,32}... | collective-permute-start | bytes 49160 | tf_op jit(solution)/shard_map/ppermute | solution.py:27
  22.0 4.6 collective-permute-start.3
  27.0 6.2 %collective-permute-start.4 = (f32[16,1,256]{2,1,0:T(1,128)S(1)}, f32[16,1,256]{2,1,0:T(1,128)S(1)}, u32[]{:S(2)}, u32[]{:S(2)}) collective-permute-start(f32[16,1,256]{2,1,0:T(1,128)S(1)} %get-tuple-element.27), channel_id=1, source_target_pairs={{4,0},{8,4},{12,8},{16,12},{20,16},{24,20},{28,24},{32,28},{36,32}... | collective-permute-start | bytes 49160 | tf_op jit(solution)/shard_map/ppermute | solution.py:27
  29.0 5.1 %collective-permute-start.5 = (f32[16,1,256]{2,1,0:T(1,128)S(1)}, f32[16,1,256]{2,1,0:T(1,128)S(1)}, u32[]{:S(2)}, u32[]{:S(2)}) collective-permute-start(f32[16,1,256]{2,1,0:T(1,128)S(1)} %get-tuple-element.28), channel_id=1, source_target_pairs={{0,4},{4,8},{8,12},{12,16},{16,20},{20,24},{24,28},{28,32},{32,36}... | collective-permute-start | bytes 49160 | tf_op jit(solution)/shard_map/ppermute | solution.py:25
  34.8 108.4 %copy-start.1 = (f32[4,64,128]{2,1,0:T(8,128)S(1)}, f32[4,64,128]{2,1,0:T(8,128)}, u32[]{:S(2)}) copy-start(f32[4,64,128]{2,1,0:T(8,128)} %param.10) | copy-start | bytes 393220
  164.4 118.7 %all-to-all-start = ((f32[16,256,128]{2,0,1:T(8,128)}), f32[16,256,128]{2,0,1:T(8,128)}, u32[]{:S(2)}, u32[]{:S(2)}) async-start(f32[16,256,128]{2,0,1:T(8,128)} %scatter_fusion), calls=%async_computation | async-start | bytes 4194304 | tf_op jit(solution)/shard_map/all_to_all | solution.py:99
  184.4 265.9 %all-gather.2.cloned.1.call-start = ((), (), s32[]{:S(2)}) async-start(), calls=%async_computation.2 | async-start | bytes 3932160 | tf_op jit(solution)/shard_map/all_gather | solution.py:122
  184.4 90.0 %collective-permute-start.6 = (f32[16,1,256]{2,1,0:T(1,128)S(1)}, f32[16,1,256]{2,1,0:T(1,128)S(1)}, u32[]{:S(2)}, u32[]{:S(2)}) collective-permute-start(f32[16,1,256]{2,1,0:T(1,128)S(1)} %get-tuple-element.17), channel_id=1, source_target_pairs={{4,0},{8,4},{12,8},{16,12},{20,16},{24,20},{28,24},{32,28},{36,32}... | collective-permute-start | bytes 49160 | tf_op jit(solution)/shard_map/ppermute | solution.py:27
  187.3 87.1 %collective-permute-start.7 = (f32[16,1,256]{2,1,0:T(1,128)S(1)}, f32[16,1,256]{2,1,0:T(1,128)S(1)}, u32[]{:S(2)}, u32[]{:S(2)}) collective-permute-start(f32[16,1,256]{2,1,0:T(1,128)S(1)} %get-tuple-element.18), channel_id=1, source_target_pairs={{0,4},{4,8},{8,12},{12,16},{16,20},{20,24},{24,28},{28,32},{32,36}... | collective-permute-start | bytes 49160 | tf_op jit(solution)/shard_map/ppermute | solution.py:25
  283.2 42.8 %all-to-all-start.1 = ((f32[16,256,128]{2,0,1:T(8,128)}), f32[16,256,128]{2,0,1:T(8,128)S(1)}, u32[]{:S(2)}, u32[]{:S(2)}) async-start(f32[16,256,128]{2,0,1:T(8,128)} %all-to-all-done), calls=%async_computation.1 | async-start | bytes 4194304 | tf_op jit(solution)/shard_map/all_to_all | solution.py:98
Sparse Core Ops, SparseCore 0:
  276.3 63.1 all-gather.1
where the time goes:
time: 463 us; the launch traced here: 462 us
  waiting for transfers between devices  132 us (29%)
  local copies, waits for them, and re-layouts  126 us (27%)
  blocking collectives  103 us (22%)
  starting transfers between devices  52.3 us (11%)
  other arithmetic  27 us (6%)
  between operations  13.7 us (3%)
  matrix products  7.66 us (2%)
    gather x1, local copies, waits for them, and re-layouts, local(): predicted = jnp.sum(obs_weights[None] * flat[:, obs_cells], axis=1)  108 us
    psum x1, blocking collectives, local(): gram, proj = lax.psum((gram, proj), ('space', 'mem'))  103 us
    ppermute x4, waiting for transfers between devices, with_halo(): lax.ppermute(head, axis, [((i + 1) % count, i) for i in range(ends)])  84.2 us
    all_to_all x1, waiting for transfers between devices, local(): lax.all_to_all(lax.all_to_all(outgoing, 'space', split_axis=1, concat_axi...  38.6 us
    all_to_all x1, starting transfers between devices, local(): lax.all_to_all(outgoing, 'space', split_axis=1, concat_axis=1, tiled=True)  19.9 us
    ppermute x4, starting transfers between devices, with_halo(): lax.ppermute(head, axis, [((i + 1) % count, i) for i in range(ends)])  15.6 us
    ppermute x4, starting transfers between devices, with_halo(): lax.ppermute(tail, axis, [(i, (i + 1) % count) for i in range(ends)])  12.6 us
    reduce_sum x1, other arithmetic, local(): predicted = jnp.sum(obs_weights[None] * flat[:, obs_cells], axis=1)  9.81 us
  transfers between devices with their start and end apart: 11, of which 6 were waited for; matrix products, arithmetic and copies ran while one was open for 5% of the time, Pallas kernels for 0%

commit v1 on v0

v1 whole, which is shorter than its diff:
```python
import math

import jax
import jax.numpy as jnp
from jax import lax
from jax.experimental import pallas as pl
from jax.experimental.pallas import tpu as pltpu
from jax.sharding import PartitionSpec as P

M = 64
NS = 128
NM = 4
NZ = 16
GROUP = 32
LM = M // NM
ROWS = 16
COLS = 256
HALO = 4
EXT = ROWS + 2 * HALO
BLK = 16
OBS = 128
N_OBS = 8192 * 128
MESH = pl.DeviceIdType.MESH
HIGHEST = lax.Precision.HIGHEST
mass_rate = 0.2
wave_rate = 0.2
turn_rate = 0.1


def east(field):
    return pltpu.roll(field, COLS - 1, 1)


def west(field):
    return pltpu.roll(field, 1, 1)


def forecast_heights(s, S, DB, H1, U1, V1, H2):
    inside_low = jnp.where(s > 0, 1.0, 0.0).astype(jnp.float32)
    inside_high = jnp.where(s < NS - 1, 1.0, 0.0).astype(jnp.float32)

    def inside(i):
        return jnp.where(i < HALO, inside_low, jnp.where(i >= HALO + ROWS, inside_high, 1.0))

    groups = [slice(0, 8), slice(8, 16)]
    for i in range(HALO):
        DB[i] = DB[i] * inside_low
        DB[HALO + ROWS + i] = DB[HALO + ROWS + i] * inside_high

    @pl.loop(1, EXT - 1)
    def _(i):
        keep = inside(i)
        for g in groups:
            flux = DB[i] * S[2, i, g]
            change = DB[i + 1] * S[1, i + 1, g] - DB[i - 1] * S[1, i - 1, g] + (east(flux) - west(flux))
            H1[i, g] = (S[0, i, g] - mass_rate * change) * keep

    @pl.loop(2, EXT - 2)
    def _(i):
        for g in groups:
            u, v, h = S[1, i, g], S[2, i, g], H1[i, g]
            U1[i, g] = u - wave_rate * (H1[i + 1, g] - H1[i - 1, g]) + turn_rate * v
            V1[i, g] = v - wave_rate * (east(h) - west(h)) - turn_rate * u

    @pl.loop(3, EXT - 3)
    def _(i):
        keep = inside(i)
        for g in groups:
            flux = DB[i] * V1[i, g]
            change = DB[i + 1] * U1[i + 1, g] - DB[i - 1] * U1[i - 1, g] + (east(flux) - west(flux))
            H2[i, g] = (H1[i, g] - mass_rate * change) * keep


def pack_block(yb, fc, packed, inverse):
    top = lax.fori_loop(
        0, ROWS, lambda r, t: jnp.maximum(t, jnp.abs(fc[yb, 0, r])), jnp.zeros((LM, COLS), jnp.float32)
    )
    top = jnp.maximum(jnp.max(top, axis=1, keepdims=True), 1e-30)
    scale = 32000.0 / top
    inverse[yb] = jnp.broadcast_to(top * (1.0 / 32000.0), (LM, OBS))

    @pl.loop(0, ROWS)
    def _(r):
        q = jnp.floor(fc[yb, 0, r] * scale + 0.5).astype(jnp.int32)
        packed[yb, r] = (q[0:8] << 16) | (q[8:16] & 0xFFFF)


def interpolate(blocks, packed, inverse, cells, weights, pred):
    @pl.loop(0, BLK)
    def _(b):
        @pl.loop(0, 2)
        def _(half):
            lane, chunk, weight = [], [], []
            for k in range(2):
                cell = jnp.broadcast_to(cells[half * 2 + k, pl.ds(b, 1), :], (8, OBS))
                lane.append(cell & (OBS - 1))
                chunk.append(cell >> 7)
                weight.append(jnp.broadcast_to(weights[half * 2 + k, pl.ds(b, 1), :], (8, OBS)))
            held = [[jnp.zeros((8, OBS), jnp.int32) for _ in blocks] for _ in range(2)]
            for c in range(ROWS * COLS // OBS):
                row, col = c // 2, (c % 2) * OBS
                here = [chunk[k] == c for k in range(2)]
                for g, yb in enumerate(blocks):
                    values = packed[yb, row, :, col : col + OBS]
                    for k in range(2):
                        found = jnp.take_along_axis(values, lane[k], axis=1, mode="promise_in_bounds")
                        held[k][g] = jnp.where(here[k], found, held[k][g])
            for g, yb in enumerate(blocks):
                high = sum((held[k][g] >> 16).astype(jnp.float32) * weight[k] for k in range(2))
                low = sum(((held[k][g] << 16) >> 16).astype(jnp.float32) * weight[k] for k in range(2))
                part = jnp.concatenate([high, low], axis=0) * inverse[yb]

                @pl.when(half == 0)
                def _():
                    pred[yb, b] = part

                @pl.when(half == 1)
                def _():
                    pred[yb, b] = pred[yb, b] + part


def main_kernel(
    target, state, depth, cells_hbm, weights_hbm, values, precisions, fc, total,
    st, dp, cells, weights, S, DB, H1, U1, V1, H2, packed, inverse, pred, X, tab_v, tab_p, Gs, rs, zs, zb, ga,
    load_sem, halo_send, halo_recv, ag_send, ag_recv, tab_send, tab_recv, red_send, red_recv,
):
    s = lax.axis_index("space")
    y = lax.axis_index("mem")
    core = s % 2
    z = (s // 2) % NZ
    x = s // (2 * NZ)
    y_low, y_high, y_far = (y + 3) % NM, (y + 1) % NM, (y + 2) % NM
    place = (x * NM + y) * 2 + core

    def member_of(q):
        return ((q // 8) * (2 * NZ) + z * 2 + q % 2, (q // 2) % NM)

    loads = [
        pltpu.make_async_copy(state.at[:, pl.ds(0, OBS)], st.at[0], load_sem.at[0]),
        pltpu.make_async_copy(state.at[:, pl.ds(OBS, OBS)], st.at[1], load_sem.at[6]),
        pltpu.make_async_copy(depth, dp, load_sem.at[1]),
        pltpu.make_async_copy(cells_hbm.at[:, pl.ds(pl.multiple_of(y * BLK, BLK), BLK)], cells, load_sem.at[2]),
        pltpu.make_async_copy(weights_hbm.at[:, pl.ds(pl.multiple_of(y * BLK, BLK), BLK)], weights, load_sem.at[3]),
    ]
    for load in loads:
        load.start()

    barrier = pltpu.get_barrier_semaphore()

    @pl.loop(1, NS)
    def _(i):
        pl.semaphore_signal(barrier, inc=1, device_id=((s + i) % NS, y), device_id_type=MESH)

    @pl.loop(0, 3 * 8)
    def _(i):
        k = i % 8
        peer = ((k // 2) * (2 * NZ) + z * 2 + k % 2, (y + 1 + i // 8) % NM)
        pl.semaphore_signal(barrier, inc=1, device_id=peer, device_id_type=MESH)

    X[M : 2 * M] = jnp.zeros((M, BLK * OBS), jnp.float32)
    for load in loads[:3]:
        load.wait()
    for f in range(3):
        for r in range(ROWS):
            for c in range(2):
                S[f, HALO + r, :, c * OBS : (c + 1) * OBS] = st[c, pl.ds(f * ROWS + r, LM, stride=3 * ROWS), :]
    for r in range(ROWS):
        DB[HALO + r] = jnp.broadcast_to(dp[pl.ds(r, 1), :], (8, COLS))
    pl.semaphore_wait(barrier, NS - 1 + 3 * 8)

    left, right = (s + NS - 1) % NS, (s + 1) % NS
    halos = []
    for n, (peer, src, dst) in enumerate(((left, HALO, HALO + ROWS), (right, ROWS, 0))):
        for k, (buf, src_ref, dst_ref) in enumerate(
            (
                (S, S.at[:, pl.ds(src, HALO)], S.at[:, pl.ds(dst, HALO)]),
                (DB, DB.at[pl.ds(src, HALO)], DB.at[pl.ds(dst, HALO)]),
            )
        ):
            halos.append(
                pltpu.make_async_remote_copy(
                    src_ref=src_ref, dst_ref=dst_ref, send_sem=halo_send.at[n, k], recv_sem=halo_recv.at[n, k],
                    device_id=(peer, y), device_id_type=MESH,
                )
            )
            halos[-1].start()
    for halo in halos:
        halo.wait()

    own_v = pltpu.make_async_copy(values.at[0, s], tab_v.at[s], load_sem.at[4])
    own_p = pltpu.make_async_copy(precisions.at[0, s], tab_p.at[s], load_sem.at[5])
    own_v.start()
    own_p.start()

    @pl.loop(1, NS)
    def _(i):
        peer = (s + i) % NS
        for k, (src, tab) in enumerate(((values, tab_v), (precisions, tab_p))):
            pltpu.make_async_remote_copy(
                src_ref=src.at[0, peer], dst_ref=tab.at[s], send_sem=tab_send.at[k], recv_sem=tab_recv.at[k],
                device_id=(peer, y), device_id_type=MESH,
            ).start()

    forecast_heights(s, S, DB, H1, U1, V1, H2)

    @pl.loop(0, ROWS)
    def _(r):
        fc[y, 0, r] = H2[HALO + r]

    def share(src, dst, n, peer):
        return pltpu.make_async_remote_copy(
            src_ref=src, dst_ref=dst, send_sem=ag_send.at[n], recv_sem=ag_recv.at[n],
            device_id=(s, peer), device_id_type=MESH,
        )

    up_h = share(H2.at[pl.ds(HALO, ROWS)], fc.at[y, 0], 0, y_high)
    down_h = share(H2.at[pl.ds(HALO, ROWS)], fc.at[y, 0], 1, y_low)
    up_h.start()
    down_h.start()

    @pl.loop(HALO, HALO + ROWS)
    def _(i):
        u, v, h = U1[i], V1[i], H2[i]
        fc[y, 1, i - HALO] = u - wave_rate * (H2[i + 1] - H2[i - 1]) + turn_rate * v
        fc[y, 2, i - HALO] = v - wave_rate * (east(h) - west(h)) - turn_rate * u

    loads[3].wait()
    loads[4].wait()
    pack_block(y, fc, packed, inverse)
    interpolate([y], packed, inverse, cells, weights, pred)
    up_h.wait()
    down_h.wait()
    half = ROWS // 2
    pass_up = share(fc.at[y_low, 0, pl.ds(0, half)], fc.at[y_low, 0, pl.ds(0, half)], 2, y_high)
    pass_down = share(fc.at[y_high, 0, pl.ds(half, half)], fc.at[y_high, 0, pl.ds(half, half)], 3, y_low)
    pass_up.start()
    pass_down.start()
    up_w = share(fc.at[y, pl.ds(1, 2)], fc.at[y, pl.ds(1, 2)], 4, y_high)
    down_w = share(fc.at[y, pl.ds(1, 2)], fc.at[y, pl.ds(1, 2)], 5, y_low)
    up_w.start()
    down_w.start()
    pack_block(y_low, fc, packed, inverse)
    pack_block(y_high, fc, packed, inverse)
    pass_up.wait()
    pass_down.wait()
    pack_block(y_far, fc, packed, inverse)
    interpolate([y_low, y_high, y_far], packed, inverse, cells, weights, pred)

    own_v.wait()
    own_p.wait()
    for k, tab in enumerate((tab_v, tab_p)):
        everyone = tab.at[pl.ds(0, NS - 1)]
        pltpu.make_async_copy(everyone, everyone, tab_recv.at[k]).wait()
        pltpu.make_async_copy(everyone, everyone, tab_send.at[k]).wait()

    scale = math.sqrt((M - 1) / N_OBS)

    @pl.loop(0, BLK)
    def _(b):
        t = target[y * BLK + b]
        seen = tab_v[t // 2, pl.ds(t % 2, 1), :]
        factor = tab_p[t // 2, pl.ds(t % 2, 1), :] * scale
        parts = [pred[yb, b] for yb in range(NM)]
        middle = jnp.sum(parts[0] + parts[1] + parts[2] + parts[3], axis=0, keepdims=True) * (1.0 / M)
        at = pl.ds(pl.multiple_of(b * OBS, OBS), OBS)
        for yb in range(NM):
            X[yb * LM : (yb + 1) * LM, at] = (parts[yb] - middle) * factor
        X[M : M + 1, at] = (seen - middle) * factor

    gram = lax.dot_general(
        X[0:M], X[...], (((1,), (1,)), ((), ())), precision=HIGHEST, preferred_element_type=jnp.float32
    )
    for q in range(GROUP):
        Gs[q] = gram[2 * q : 2 * q + 2]

    @pl.loop(1, GROUP)
    def _(i):
        q = (place + i) % GROUP
        pltpu.make_async_remote_copy(
            src_ref=Gs.at[q], dst_ref=rs.at[place], send_sem=red_send.at[0], recv_sem=red_recv.at[0],
            device_id=member_of(q), device_id_type=MESH,
        ).start()

    rs[place] = Gs[place]
    others = rs.at[pl.ds(0, GROUP - 1)]
    pltpu.make_async_copy(others, others, red_recv.at[0]).wait()
    mine = rs[0]
    for q in range(1, GROUP):
        mine = mine + rs[q]
    zs[...] = mine
    zb[z] = mine

    @pl.loop(1, NZ)
    def _(i):
        other = (z + i) % NZ
        pltpu.make_async_remote_copy(
            src_ref=zs, dst_ref=zb.at[z], send_sem=red_send.at[1], recv_sem=red_recv.at[1],
            device_id=(x * (2 * NZ) + other * 2 + core, y), device_id_type=MESH,
        ).start()

    others_z = zb.at[pl.ds(0, NZ - 1)]
    pltpu.make_async_copy(others_z, others_z, red_recv.at[1]).wait()
    mine = zb[0]
    for q in range(1, NZ):
        mine = mine + zb[q]
    ga[place] = mine

    @pl.loop(1, GROUP)
    def _(i):
        q = (place + i) % GROUP
        pltpu.make_async_remote_copy(
            src_ref=ga.at[place], dst_ref=ga.at[place], send_sem=red_send.at[2], recv_sem=red_recv.at[2],
            device_id=member_of(q), device_id_type=MESH,
        ).start()

    up_w.wait()
    down_w.wait()
    pass_u = share(fc.at[y_low, 1], fc.at[y_low, 1], 6, y_high)
    pass_v = share(fc.at[y_high, 2], fc.at[y_high, 2], 7, y_low)
    pass_u.start()
    pass_v.start()
    pltpu.make_async_copy(others, others, red_send.at[0]).wait()
    pltpu.make_async_copy(others_z, others_z, red_send.at[1]).wait()
    others_a = ga.at[pl.ds(0, GROUP - 1)]
    pltpu.make_async_copy(others_a, others_a, red_recv.at[2]).wait()
    pltpu.make_async_copy(others_a, others_a, red_send.at[2]).wait()
    for q in range(GROUP):
        total[2 * q : 2 * q + 2] = ga[q]
    pass_u.wait()
    pass_v.wait()


def combine_kernel(total, fc, out, inv_ref, held, sem):
    y = lax.axis_index("mem")
    g = total[...]
    row = lax.broadcasted_iota(jnp.int32, (M, 2 * M), 0)
    lane = lax.broadcasted_iota(jnp.int32, (M, 2 * M), 1)
    proj = g[:, M : M + 1]
    eye = jnp.where(lane == row + M, 1.0, 0.0)
    work = jnp.where(lane < M, g + jnp.where(lane == row, float(M - 1), 0.0), eye)
    for k in range(M - 1):
        pivot = work[k : k + 1, :]
        ratio = work[:, k : k + 1] * (1.0 / work[k : k + 1, k : k + 1])
        work = work - jnp.where(row > k, ratio * pivot, 0.0)
    diagonal = jnp.sum(jnp.where(lane == row, work, 0.0), axis=1, keepdims=True)
    lower_inv = work[:, M:] * (1.0 / jnp.sqrt(diagonal))
    inv_ref[...] = lower_inv
    square = jnp.where(row[:, :M] == lane[:, :M], 1.0, 0.0)
    proj_row = jnp.broadcast_to(jnp.sum(square * proj, axis=0, keepdims=True), (8, M))
    first = lax.dot_general(
        proj_row, lower_inv, (((1,), (1,)), ((), ())), precision=HIGHEST, preferred_element_type=jnp.float32
    )
    mean_weights = jnp.dot(first, lower_inv, precision=HIGHEST, preferred_element_type=jnp.float32)[0:1]
    coef = mean_weights + math.sqrt(M - 1) * inv_ref[pl.ds(pl.multiple_of(y * LM, LM), LM), :]
    mixing = coef + (1.0 - jnp.sum(coef, axis=1, keepdims=True)) * (1.0 / M)
    for f in range(3):

        @pl.loop(0, ROWS)
        def _(r):
            prior = jnp.concatenate([fc[yb, f, r] for yb in range(NM)], axis=0)
            new = jnp.dot(mixing, prior, precision=HIGHEST, preferred_element_type=jnp.float32)
            for c in range(2):
                held[c, pl.ds(f * ROWS + r, LM, stride=3 * ROWS), :] = new[:, c * OBS : (c + 1) * OBS]

    stores = [pltpu.make_async_copy(held.at[c], out.at[:, pl.ds(c * OBS, OBS)], sem.at[c]) for c in range(2)]
    for store in stores:
        store.start()
    for store in stores:
        store.wait()


def local(state, depth, obs_cells, obs_weights, owner_map, obs_values, obs_precision):
    owners = owner_map[:, 0]
    same = (owners[:, None] == owners[None, :]).astype(jnp.int32)
    order = jnp.arange(owners.shape[0], dtype=jnp.int32)
    earlier = (order[:, None] < order[None, :]).astype(jnp.int32)
    target = owners * 2 + jnp.sum(same * earlier, axis=0)
    any_space = pl.BlockSpec(memory_space=pl.ANY)
    f32 = jnp.float32
    fc, total = pl.pallas_call(
        main_kernel,
        name="forecast_and_reduce",
        out_shape=(
            jax.ShapeDtypeStruct((NM, 3, ROWS, LM, COLS), f32),
            jax.ShapeDtypeStruct((M, 2 * M), f32),
        ),
        in_specs=[pl.BlockSpec(memory_space=pltpu.SMEM)] + [any_space] * 6,
        out_specs=(pl.BlockSpec(memory_space=pltpu.VMEM), pl.BlockSpec(memory_space=pltpu.VMEM)),
        scratch_shapes=[
            pltpu.VMEM((2, LM * 3 * ROWS, OBS), f32),
            pltpu.VMEM((ROWS, COLS), f32),
            pltpu.VMEM((4, BLK, OBS), jnp.int32),
            pltpu.VMEM((4, BLK, OBS), f32),
            pltpu.VMEM((3, EXT, LM, COLS), f32),
            pltpu.VMEM((EXT, 8, COLS), f32),
            pltpu.VMEM((EXT, LM, COLS), f32),
            pltpu.VMEM((EXT, LM, COLS), f32),
            pltpu.VMEM((EXT, LM, COLS), f32),
            pltpu.VMEM((EXT, LM, COLS), f32),
            pltpu.VMEM((NM, ROWS, 8, COLS), jnp.int32),
            pltpu.VMEM((NM, LM, OBS), f32),
            pltpu.VMEM((NM, BLK, LM, OBS), f32),
            pltpu.VMEM((2 * M, BLK * OBS), f32),
            pltpu.VMEM((NS, 2, OBS), f32),
            pltpu.VMEM((NS, 2, OBS), f32),
            pltpu.VMEM((GROUP, 2, 2 * M), f32),
            pltpu.VMEM((GROUP, 2, 2 * M), f32),
            pltpu.VMEM((2, 2 * M), f32),
            pltpu.VMEM((NZ, 2, 2 * M), f32),
            pltpu.VMEM((GROUP, 2, 2 * M), f32),
            pltpu.SemaphoreType.DMA((7,)),
            pltpu.SemaphoreType.DMA((2, 2)),
            pltpu.SemaphoreType.DMA((2, 2)),
            pltpu.SemaphoreType.DMA((8,)),
            pltpu.SemaphoreType.DMA((8,)),
            pltpu.SemaphoreType.DMA((2,)),
            pltpu.SemaphoreType.DMA((2,)),
            pltpu.SemaphoreType.DMA((3,)),
            pltpu.SemaphoreType.DMA((3,)),
        ],
        compiler_params=pltpu.CompilerParams(collective_id=0, has_side_effects=True, vmem_limit_bytes=40 << 20),
    )(target, state.reshape(LM * 3 * ROWS, COLS), depth, obs_cells, obs_weights, obs_values, obs_precision)
    vmem = pl.BlockSpec(memory_space=pltpu.VMEM)
    out = pl.pallas_call(
        combine_kernel,
        name="combine_members",
        out_shape=jax.ShapeDtypeStruct((LM * 3 * ROWS, COLS), f32),
        in_specs=[vmem, vmem],
        out_specs=any_space,
        scratch_shapes=[
            pltpu.VMEM((M, M), f32),
            pltpu.VMEM((2, LM * 3 * ROWS, OBS), f32),
            pltpu.SemaphoreType.DMA((2,)),
        ],
        compiler_params=pltpu.CompilerParams(vmem_limit_bytes=40 << 20),
    )(total, fc)
    return out.reshape(LM, 3, ROWS, COLS)


def solution(mesh):
    return jax.shard_map(
        local,
        mesh=mesh,
        in_specs=(
            P("mem", None, "space", None),
            P("space", None),
            P(None, "space", None),
            P(None, "space", None),
            P("space", None),
            P("space", None, None, None),
            P("space", None, None, None),
        ),
        out_specs=P("mem", None, "space", None),
        check_vma=False,
    )
```

time: 463 us -> 98.8 us (0.21)
  waiting for transfers between devices: 132 us -> 0 us
  local copies, waits for them, and re-layouts: 126 us -> 5.46 us
  blocking collectives: 103 us -> 0 us
  Pallas kernels: 0 us -> 91.6 us
  starting transfers between devices: 52.3 us -> 0 us
  other arithmetic: 27 us -> 1.48 us
  between operations: 13.7 us -> 0.02 us
  matrix products: 7.66 us -> 0 us
    gather x1 -> x0, local copies, waits for them, and re-layouts: 108 us -> none  [local(): predicted = jnp.sum(obs_weights[None] * flat[:, obs_cells], axis=1)]
    psum x1 -> x0, blocking collectives: 103 us -> none  [local(): gram, proj = lax.psum((gram, proj), ('space', 'mem'))]
    pallas_call x0 -> x2, Pallas kernels: none -> 91.6 us  [the longest x1 77.6 us: local(): pl.pallas_call(main_kernel, name='forecast_and_reduce', out_shape=(jax.Sh...]
    ppermute x8 -> x0, waiting for transfers between devices: 86.4 us -> none  [the longest x4 84.2 us: with_halo(): lax.ppermute(head, axis, [((i + 1) % count, i) for i in range(ends)])]
    all_to_all x2 -> x0, waiting for transfers between devices: 45.6 us -> none  [the longest x1 38.6 us: local(): lax.all_to_all(lax.all_to_all(outgoing, 'space', split_axis=1, concat_axi...]
    ppermute x8 -> x0, starting transfers between devices: 28.2 us -> none  [the longest x4 15.6 us: with_halo(): lax.ppermute(head, axis, [((i + 1) % count, i) for i in range(ends)])]
    all_to_all x2 -> x0, starting transfers between devices: 24.1 us -> none  [the longest x1 19.9 us: local(): lax.all_to_all(outgoing, 'space', split_axis=1, concat_axis=1, tiled=True)]
    another operation x7 -> x0, other arithmetic: 12.2 us -> none  [the longest x3 6.52 us: local(): lower = jnp.linalg.cholesky((M - 1) * eye + gram)]
  transfers between devices with their start and end apart: 11 -> 0, of which waited for: 6 -> 0; matrix products, arithmetic and copies ran while one was open for 5% -> 0% of each run, Pallas kernels for 0% -> 0%
where the time goes in v1:
time: 98.8 us; the launch traced here: 98.5 us
  Pallas kernels  91.6 us (93%)
  local copies, waits for them, and re-layouts  5.46 us (6%)
  other arithmetic  1.48 us (1%)
    pallas_call x1, Pallas kernels, local(): pl.pallas_call(main_kernel, name='forecast_and_reduce', out_shape=(jax.Sh...  77.6 us
    pallas_call x1, Pallas kernels, local(): pl.pallas_call(combine_kernel, name='combine_members', out_shape=jax.Shap...  14 us
    unnamed x12, local copies, waits for them, and re-layouts  5.46 us

profile of v1, /device:TPU:1, one launch (start us, length us, event | category | flops | bytes accessed | tf_op | source)
XLA Modules:
  0.0 98.5 jit_solution(6805198470557833929)
XLA Ops:
  0.0 0.8 select_reduce_fusion
  0.8 0.7 multiply_add_fusion.target
  1.5 0.0 copy-start
  1.5 1.1 %copy-done = f32[16,3,16,256]{3,2,1,0:T(8,128)S(1)} copy-done((f32[16,3,16,256]{3,2,1,0:T(8,128)S(1)}, f32[16,3,16,256]{3,2,1,0:T(8,128)}, u32[]{:S(2)}) %copy-start) | copy-done | bytes 786456
  2.6 0.0 copy-start.1
  2.6 0.9 copy-done.1
  3.5 0.0 copy-start.2
  3.5 0.9 copy-done.2
  4.4 0.0 copy-start.3
  4.4 0.9 copy-done.3
  5.3 0.0 copy-start.4
  5.3 0.9 copy-done.4
  6.2 0.0 copy-start.5
  6.2 0.7 copy-done.5
  7.0 77.6 %forecast_and_reduce.1 = (f32[4,3,16,16,256]{4,3,2,1,0:T(8,128)S(1)}, f32[64,128]{1,0:T(8,128)S(1)}) custom-call(s32[64]{0:T(128)S(1)} %multiply_add_fusion.target, f32[768,256]{1,0:T(8,128)S(1)} %bitcast.4, f32[16,256]{1,0:T(8,128)S(1)} %copy-done.5, s32[4,64,128]{2,1,0:T(8,128)S(1)} %copy-done.1, f32[4,64,128]{2,1,0:T(8,128)S(1)} %copy-done.2, ...), custom_call_target="tpu_custom_call" | custom-call | tf_op jit(solution)/shard_map/forecast_and_reduce/pallas_call | solution.py:380
  84.5 14.0 %combine_members.1 = f32[768,256]{1,0:T(8,128)} custom-call(f32[64,128]{1,0:T(8,128)S(1)} %get-tuple-element.7.total, f32[4,3,16,16,256]{4,3,2,1,0:T(8,128)S(1)} %get-tuple-element.8.fc), custom_call_target="tpu_custom_call" | custom-call | tf_op jit(solution)/shard_map/combine_members/pallas_call | solution.py:424
Async XLA Ops:
  1.5 1.1 %copy-start = (f32[16,3,16,256]{3,2,1,0:T(8,128)S(1)}, f32[16,3,16,256]{3,2,1,0:T(8,128)}, u32[]{:S(2)}) copy-start(f32[16,3,16,256]{3,2,1,0:T(8,128)} %param.7) | copy-start | bytes 2359300
  2.6 0.9 copy-start.1
  3.5 0.9 copy-start.2
  4.4 0.9 copy-start.3
  5.3 0.9 copy-start.4
  6.2 0.7 copy-start.5

commit v2 on v1

--- a/solution.py
+++ b/solution.py
@@ -20,6 +20,9 @@
 BLK = 16
 OBS = 128
 N_OBS = 8192 * 128
+GROUPS = (slice(0, 8), slice(8, 16))
+EAST, HEIGHT, NORTH = 0, 1, 2
+FIELD = (HEIGHT, EAST, NORTH)
 MESH = pl.DeviceIdType.MESH
 HIGHEST = lax.Precision.HIGHEST
 mass_rate = 0.2
@@ -35,40 +38,25 @@
     return pltpu.roll(field, 1, 1)
 
 
-def forecast_heights(s, S, DB, H1, U1, V1, H2):
-    inside_low = jnp.where(s > 0, 1.0, 0.0).astype(jnp.float32)
-    inside_high = jnp.where(s < NS - 1, 1.0, 0.0).astype(jnp.float32)
-
-    def inside(i):
-        return jnp.where(i < HALO, inside_low, jnp.where(i >= HALO + ROWS, inside_high, 1.0))
-
-    groups = [slice(0, 8), slice(8, 16)]
-    for i in range(HALO):
-        DB[i] = DB[i] * inside_low
-        DB[HALO + ROWS + i] = DB[HALO + ROWS + i] * inside_high
-
-    @pl.loop(1, EXT - 1)
-    def _(i):
-        keep = inside(i)
-        for g in groups:
-            flux = DB[i] * S[2, i, g]
-            change = DB[i + 1] * S[1, i + 1, g] - DB[i - 1] * S[1, i - 1, g] + (east(flux) - west(flux))
-            H1[i, g] = (S[0, i, g] - mass_rate * change) * keep
-
-    @pl.loop(2, EXT - 2)
-    def _(i):
-        for g in groups:
-            u, v, h = S[1, i, g], S[2, i, g], H1[i, g]
-            U1[i, g] = u - wave_rate * (H1[i + 1, g] - H1[i - 1, g]) + turn_rate * v
-            V1[i, g] = v - wave_rate * (east(h) - west(h)) - turn_rate * u
-
-    @pl.loop(3, EXT - 3)
-    def _(i):
-        keep = inside(i)
-        for g in groups:
-            flux = DB[i] * V1[i, g]
-            change = DB[i + 1] * U1[i + 1, g] - DB[i - 1] * U1[i - 1, g] + (east(flux) - west(flux))
-            H2[i, g] = (H1[i, g] - mass_rate * change) * keep
+def height_step(i, keep, S, DB, H1):
+    for g in GROUPS:
+        flux = DB[i] * S[NORTH, i, g]
+        change = DB[i + 1] * S[EAST, i + 1, g] - DB[i - 1] * S[EAST, i - 1, g] + (east(flux) - west(flux))
+        H1[i, g] = (S[HEIGHT, i, g] - mass_rate * change) * keep
+
+
+def wind_step(i, S, H1, U1, V1):
+    for g in GROUPS:
+        u, v, h = S[EAST, i, g], S[NORTH, i, g], H1[i, g]
+        U1[i, g] = u - wave_rate * (H1[i + 1, g] - H1[i - 1, g]) + turn_rate * v
+        V1[i, g] = v - wave_rate * (east(h) - west(h)) - turn_rate * u
+
+
+def second_height(i, keep, DB, H1, U1, V1, H2):
+    for g in GROUPS:
+        flux = DB[i] * V1[i, g]
+        change = DB[i + 1] * U1[i + 1, g] - DB[i - 1] * U1[i - 1, g] + (east(flux) - west(flux))
+        H2[i, g] = (H1[i, g] - mass_rate * change) * keep
 
 
 def pack_block(yb, fc, packed, inverse):
@@ -86,10 +74,10 @@
 
 
 def interpolate(blocks, packed, inverse, cells, weights, pred):
-    @pl.loop(0, BLK)
-    def _(b):
-        @pl.loop(0, 2)
-        def _(half):
+    for half in range(2):
+
+        @pl.loop(0, BLK)
+        def _(b):
             lane, chunk, weight = [], [], []
             for k in range(2):
                 cell = jnp.broadcast_to(cells[half * 2 + k, pl.ds(b, 1), :], (8, OBS))
@@ -109,20 +97,13 @@
                 high = sum((held[k][g] >> 16).astype(jnp.float32) * weight[k] for k in range(2))
                 low = sum(((held[k][g] << 16) >> 16).astype(jnp.float32) * weight[k] for k in range(2))
                 part = jnp.concatenate([high, low], axis=0) * inverse[yb]
-
-                @pl.when(half == 0)
-                def _():
-                    pred[yb, b] = part
-
-                @pl.when(half == 1)
-                def _():
-                    pred[yb, b] = pred[yb, b] + part
+                pred[yb, b] = part if half == 0 else pred[yb, b] + part
 
 
 def main_kernel(
-    target, state, depth, cells_hbm, weights_hbm, values, precisions, fc, total,
-    st, dp, cells, weights, S, DB, H1, U1, V1, H2, packed, inverse, pred, X, tab_v, tab_p, Gs, rs, zs, zb, ga,
-    load_sem, halo_send, halo_recv, ag_send, ag_recv, tab_send, tab_recv, red_send, red_recv,
+    owners_hbm, state, depth, cells_hbm, weights_hbm, values, precisions, fc, total,
+    owners, target, st, dp, cells, weights, S, DB, H1, U1, V1, H2, packed, inverse, pred, X, tab_v, tab_p, Gs, rs, zs, zb, ga,
+    load_sem, halo_send, halo_recv, ag_send, ag_recv, tab_send, tab_recv, red_send, red_recv, round_sem,
 ):
     s = lax.axis_index("space")
     y = lax.axis_index("mem")
@@ -131,64 +112,148 @@
     x = s // (2 * NZ)
     y_low, y_high, y_far = (y + 3) % NM, (y + 1) % NM, (y + 2) % NM
     place = (x * NM + y) * 2 + core
+    left, right = (s + NS - 1) % NS, (s + 1) % NS
 
     def member_of(q):
         return ((q // 8) * (2 * NZ) + z * 2 + q % 2, (q // 2) % NM)
 
+    def along_z(step):
+        return (x * (2 * NZ) + ((z + step + NZ) % NZ) * 2 + core, y)
+
+    def along_x(step):
+        return (((x + step + 4) % 4) * (2 * NZ) + z * 2 + core, y)
+
+    def along_y(step):
+        return (s, (y + step + NM) % NM)
+
+    partner = (s + 1 - 2 * core, y)
+    own_rows = pl.ds(pl.multiple_of(y * BLK, BLK), BLK)
     loads = [
         pltpu.make_async_copy(state.at[:, pl.ds(0, OBS)], st.at[0], load_sem.at[0]),
-        pltpu.make_async_copy(state.at[:, pl.ds(OBS, OBS)], st.at[1], load_sem.at[6]),
-        pltpu.make_async_copy(depth, dp, load_sem.at[1]),
-        pltpu.make_async_copy(cells_hbm.at[:, pl.ds(pl.multiple_of(y * BLK, BLK), BLK)], cells, load_sem.at[2]),
-        pltpu.make_async_copy(weights_hbm.at[:, pl.ds(pl.multiple_of(y * BLK, BLK), BLK)], weights, load_sem.at[3]),
+        pltpu.make_async_copy(state.at[:, pl.ds(OBS, OBS)], st.at[1], load_sem.at[1]),
+        pltpu.make_async_copy(depth, dp, load_sem.at[2]),
+        pltpu.make_async_copy(cells_hbm.at[:, own_rows], cells, load_sem.at[3]),
+        pltpu.make_async_copy(weights_hbm.at[:, own_rows], weights, load_sem.at[4]),
+        pltpu.make_async_copy(owners_hbm, owners, load_sem.at[5]),
     ]
     for load in loads:
         load.start()
 
     barrier = pltpu.get_barrier_semaphore()
-
-    @pl.loop(1, NS)
-    def _(i):
-        pl.semaphore_signal(barrier, inc=1, device_id=((s + i) % NS, y), device_id_type=MESH)
-
-    @pl.loop(0, 3 * 8)
-    def _(i):
-        k = i % 8
-        peer = ((k // 2) * (2 * NZ) + z * 2 + k % 2, (y + 1 + i // 8) % NM)
+    cross = (left + core * (right - left), y)
+    near = [partner, cross, along_z(1), along_z(-1), along_x(1), along_x(-1), along_y(1), along_y(-1)]
+    for peer in near:
         pl.semaphore_signal(barrier, inc=1, device_id=peer, device_id_type=MESH)
 
-    X[M : 2 * M] = jnp.zeros((M, BLK * OBS), jnp.float32)
+    rounds = [
+        (along_z(1), along_z(-1)),
+        (along_z(2), along_z(-2)),
+        (along_z(4), along_z(-4)),
+        (partner,),
+        (along_x(1), along_x(-1)),
+        (along_x(1), along_x(-1)),
+        (along_y(1), along_y(-1)),
+        (along_y(1), along_y(-1)),
+    ]
+
+    def tell(n):
+        for peer in rounds[n]:
+            pl.semaphore_signal(round_sem.at[n], inc=1, device_id=peer, device_id_type=MESH)
+
+    def hear(n):
+        pl.semaphore_wait(round_sem.at[n], len(rounds[n]))
+
     for load in loads[:3]:
         load.wait()
     for f in range(3):
         for r in range(ROWS):
             for c in range(2):
-                S[f, HALO + r, :, c * OBS : (c + 1) * OBS] = st[c, pl.ds(f * ROWS + r, LM, stride=3 * ROWS), :]
+                S[FIELD[f], HALO + r, :, c * OBS : (c + 1) * OBS] = st[c, pl.ds(f * ROWS + r, LM, stride=3 * ROWS), :]
     for r in range(ROWS):
         DB[HALO + r] = jnp.broadcast_to(dp[pl.ds(r, 1), :], (8, COLS))
-    pl.semaphore_wait(barrier, NS - 1 + 3 * 8)
-
-    left, right = (s + NS - 1) % NS, (s + 1) % NS
+    pl.semaphore_wait(barrier, len(near))
+
     halos = []
     for n, (peer, src, dst) in enumerate(((left, HALO, HALO + ROWS), (right, ROWS, 0))):
-        for k, (buf, src_ref, dst_ref) in enumerate(
-            (
-                (S, S.at[:, pl.ds(src, HALO)], S.at[:, pl.ds(dst, HALO)]),
-                (DB, DB.at[pl.ds(src, HALO)], DB.at[pl.ds(dst, HALO)]),
-            )
+        for k, (buf, lead, skip, rows) in enumerate(
+            ((S, (EAST,), 0, HALO), (S, (pl.ds(HEIGHT, 2),), n, HALO - 1), (DB, (), 0, HALO))
         ):
             halos.append(
                 pltpu.make_async_remote_copy(
-                    src_ref=src_ref, dst_ref=dst_ref, send_sem=halo_send.at[n, k], recv_sem=halo_recv.at[n, k],
-                    device_id=(peer, y), device_id_type=MESH,
+                    src_ref=buf.at[(*lead, pl.ds(src + skip, rows))], dst_ref=buf.at[(*lead, pl.ds(dst + skip, rows))],
+                    send_sem=halo_send.at[n, k], recv_sem=halo_recv.at[n, k], device_id=(peer, y), device_id_type=MESH,
                 )
             )
             halos[-1].start()
+
+    tell(0)
+
+    @pl.loop(HALO + 1, HALO + ROWS - 1, unroll=2)
+    def _(i):
+        height_step(i, 1.0, S, DB, H1)
+
+    hear(0)
+    tell(1)
+
+    @pl.loop(HALO + 2, HALO + ROWS - 2, unroll=2)
+    def _(i):
+        wind_step(i, S, H1, U1, V1)
+
+    hear(1)
+    tell(2)
+
+    @pl.loop(HALO + 3, HALO + ROWS - 3, unroll=2)
+    def _(i):
+        second_height(i, 1.0, DB, H1, U1, V1, H2)
+
+    hear(2)
+    tell(3)
     for halo in halos:
         halo.wait()
 
-    own_v = pltpu.make_async_copy(values.at[0, s], tab_v.at[s], load_sem.at[4])
-    own_p = pltpu.make_async_copy(precisions.at[0, s], tab_p.at[s], load_sem.at[5])
+    inside_low = jnp.where(s > 0, 1.0, 0.0).astype(jnp.float32)
+    inside_high = jnp.where(s < NS - 1, 1.0, 0.0).astype(jnp.float32)
+    for i in range(HALO):
+        DB[i] = DB[i] * inside_low
+        DB[HALO + ROWS + i] = DB[HALO + ROWS + i] * inside_high
+    for i in range(1, 5):
+        height_step(i, inside_low if i < HALO else 1.0, S, DB, H1)
+        height_step(EXT - 1 - i, inside_high if i < HALO else 1.0, S, DB, H1)
+    hear(3)
+    tell(4)
+    for i in range(2, 6):
+        wind_step(i, S, H1, U1, V1)
+        wind_step(EXT - 1 - i, S, H1, U1, V1)
+    hear(4)
+    tell(5)
+    for i in range(3, 7):
+        second_height(i, inside_low if i < HALO else 1.0, DB, H1, U1, V1, H2)
+        second_height(EXT - 1 - i, inside_high if i < HALO else 1.0, DB, H1, U1, V1, H2)
+
+    def share(src, dst, n, peer):
+        copy = pltpu.make_async_remote_copy(
+            src_ref=src, dst_ref=dst, send_sem=ag_send.at[n], recv_sem=ag_recv.at[n],
+            device_id=(s, peer), device_id_type=MESH,
+        )
+        copy.start()
+        return copy
+
+    half = ROWS // 2
+    first, last = pl.ds(0, half), pl.ds(half, half)
+    sent_first, sent_last = H2.at[pl.ds(HALO, half)], H2.at[pl.ds(HALO + half, half)]
+    up_first = share(sent_first, fc.at[y, 0, first], 0, y_high)
+    down_first = share(sent_last, fc.at[y, 0, last], 1, y_low)
+    up_last = share(sent_last, fc.at[y, 0, last], 2, y_high)
+    down_last = share(sent_first, fc.at[y, 0, first], 3, y_low)
+
+    @pl.loop(0, ROWS, unroll=2)
+    def _(r):
+        fc[y, 0, r] = H2[HALO + r]
+
+    hear(5)
+    tell(6)
+    own_v = pltpu.make_async_copy(values.at[0, s], tab_v.at[s], load_sem.at[6])
+    own_p = pltpu.make_async_copy(precisions.at[0, s], tab_p.at[s], load_sem.at[7])
     own_v.start()
     own_p.start()
 
@@ -201,63 +266,62 @@
                 device_id=(peer, y), device_id_type=MESH,
             ).start()
 
-    forecast_heights(s, S, DB, H1, U1, V1, H2)
-
-    @pl.loop(0, ROWS)
-    def _(r):
-        fc[y, 0, r] = H2[HALO + r]
-
-    def share(src, dst, n, peer):
-        return pltpu.make_async_remote_copy(
-            src_ref=src, dst_ref=dst, send_sem=ag_send.at[n], recv_sem=ag_recv.at[n],
-            device_id=(s, peer), device_id_type=MESH,
-        )
-
-    up_h = share(H2.at[pl.ds(HALO, ROWS)], fc.at[y, 0], 0, y_high)
-    down_h = share(H2.at[pl.ds(HALO, ROWS)], fc.at[y, 0], 1, y_low)
-    up_h.start()
-    down_h.start()
-
-    @pl.loop(HALO, HALO + ROWS)
+    loads[3].wait()
+    loads[4].wait()
+    loads[5].wait()
+    pack_block(y, fc, packed, inverse)
+    interpolate([y], packed, inverse, cells, weights, pred)
+    hear(6)
+    tell(7)
+    up_first.wait_recv()
+    down_first.wait_recv()
+    pass_up = share(fc.at[y_low, 0, first], fc.at[y_low, 0, first], 4, y_high)
+    pass_down = share(fc.at[y_high, 0, last], fc.at[y_high, 0, last], 5, y_low)
+
+    @pl.loop(HALO, HALO + ROWS, unroll=2)
     def _(i):
         u, v, h = U1[i], V1[i], H2[i]
         fc[y, 1, i - HALO] = u - wave_rate * (H2[i + 1] - H2[i - 1]) + turn_rate * v
         fc[y, 2, i - HALO] = v - wave_rate * (east(h) - west(h)) - turn_rate * u
 
-    loads[3].wait()
-    loads[4].wait()
-    pack_block(y, fc, packed, inverse)
-    interpolate([y], packed, inverse, cells, weights, pred)
-    up_h.wait()
-    down_h.wait()
-    half = ROWS // 2
-    pass_up = share(fc.at[y_low, 0, pl.ds(0, half)], fc.at[y_low, 0, pl.ds(0, half)], 2, y_high)
-    pass_down = share(fc.at[y_high, 0, pl.ds(half, half)], fc.at[y_high, 0, pl.ds(half, half)], 3, y_low)
-    pass_up.start()
-    pass_down.start()
-    up_w = share(fc.at[y, pl.ds(1, 2)], fc.at[y, pl.ds(1, 2)], 4, y_high)
-    down_w = share(fc.at[y, pl.ds(1, 2)], fc.at[y, pl.ds(1, 2)], 5, y_low)
-    up_w.start()
-    down_w.start()
+    up_w = share(fc.at[y, pl.ds(1, 2)], fc.at[y, pl.ds(1, 2)], 6, y_high)
+    down_w = share(fc.at[y, pl.ds(1, 2)], fc.at[y, pl.ds(1, 2)], 7, y_low)
+
+    @pl.loop(0, BLK)
+    def _(b):
+        me = y * BLK + b
+        owner = owners[me]
+        slot = jnp.int32(0)
+        for other in range(8192 // NS):
+            slot = slot + jnp.where((owners[other] == owner) & (other < me), 1, 0)
+        target[b] = owner * 2 + slot
+
+    up_last.wait_recv()
+    down_last.wait_recv()
     pack_block(y_low, fc, packed, inverse)
     pack_block(y_high, fc, packed, inverse)
-    pass_up.wait()
-    pass_down.wait()
+    pass_up.wait_recv()
+    pass_down.wait_recv()
     pack_block(y_far, fc, packed, inverse)
     interpolate([y_low, y_high, y_far], packed, inverse, cells, weights, pred)
+    up_w.wait_recv()
+    down_w.wait_recv()
+    pass_u = share(fc.at[y_low, 1], fc.at[y_low, 1], 8, y_high)
+    pass_v = share(fc.at[y_high, 2], fc.at[y_high, 2], 9, y_low)
+    hear(7)
 
     own_v.wait()
     own_p.wait()
     for k, tab in enumerate((tab_v, tab_p)):
         everyone = tab.at[pl.ds(0, NS - 1)]
         pltpu.make_async_copy(everyone, everyone, tab_recv.at[k]).wait()
-        pltpu.make_async_copy(everyone, everyone, tab_send.at[k]).wait()
 
     scale = math.sqrt((M - 1) / N_OBS)
+    X[M : 2 * M] = jnp.zeros((M, BLK * OBS), jnp.float32)
 
     @pl.loop(0, BLK)
     def _(b):
-        t = target[y * BLK + b]
+        t = target[b]
         seen = tab_v[t // 2, pl.ds(t % 2, 1), :]
         factor = tab_p[t // 2, pl.ds(t % 2, 1), :] * scale
         parts = [pred[yb, b] for yb in range(NM)]
@@ -313,12 +377,6 @@
             device_id=member_of(q), device_id_type=MESH,
         ).start()
 
-    up_w.wait()
-    down_w.wait()
-    pass_u = share(fc.at[y_low, 1], fc.at[y_low, 1], 6, y_high)
-    pass_v = share(fc.at[y_high, 2], fc.at[y_high, 2], 7, y_low)
-    pass_u.start()
-    pass_v.start()
     pltpu.make_async_copy(others, others, red_send.at[0]).wait()
     pltpu.make_async_copy(others_z, others_z, red_send.at[1]).wait()
     others_a = ga.at[pl.ds(0, GROUP - 1)]
@@ -326,8 +384,13 @@
     pltpu.make_async_copy(others_a, others_a, red_send.at[2]).wait()
     for q in range(GROUP):
         total[2 * q : 2 * q + 2] = ga[q]
-    pass_u.wait()
-    pass_v.wait()
+    pass_u.wait_recv()
+    pass_v.wait_recv()
+    for copy in (up_first, down_first, up_last, down_last, pass_up, pass_down, up_w, down_w, pass_u, pass_v):
+        copy.wait_send()
+    for k, tab in enumerate((tab_v, tab_p)):
+        everyone = tab.at[pl.ds(0, NS - 1)]
+        pltpu.make_async_copy(everyone, everyone, tab_send.at[k]).wait()
 
 
 def combine_kernel(total, fc, out, inv_ref, held, sem):
@@ -370,12 +433,7 @@
 
 
 def local(state, depth, obs_cells, obs_weights, owner_map, obs_values, obs_precision):
-    owners = owner_map[:, 0]
-    same = (owners[:, None] == owners[None, :]).astype(jnp.int32)
-    order = jnp.arange(owners.shape[0], dtype=jnp.int32)
-    earlier = (order[:, None] < order[None, :]).astype(jnp.int32)
-    target = owners * 2 + jnp.sum(same * earlier, axis=0)
-    any_space = pl.BlockSpec(memory_space=pl.ANY)
+    any_space = pl.BlockSpec(memory_space=pltpu.HBM)
     f32 = jnp.float32
     fc, total = pl.pallas_call(
         main_kernel,
@@ -384,9 +442,11 @@
             jax.ShapeDtypeStruct((NM, 3, ROWS, LM, COLS), f32),
             jax.ShapeDtypeStruct((M, 2 * M), f32),
         ),
-        in_specs=[pl.BlockSpec(memory_space=pltpu.SMEM)] + [any_space] * 6,
+        in_specs=[any_space] * 7,
         out_specs=(pl.BlockSpec(memory_space=pltpu.VMEM), pl.BlockSpec(memory_space=pltpu.VMEM)),
         scratch_shapes=[
+            pltpu.SMEM((8192 // NS,), jnp.int32),
+            pltpu.SMEM((BLK,), jnp.int32),
             pltpu.VMEM((2, LM * 3 * ROWS, OBS), f32),
             pltpu.VMEM((ROWS, COLS), f32),
             pltpu.VMEM((4, BLK, OBS), jnp.int32),
@@ -408,18 +468,27 @@
             pltpu.VMEM((2, 2 * M), f32),
             pltpu.VMEM((NZ, 2, 2 * M), f32),
             pltpu.VMEM((GROUP, 2, 2 * M), f32),
-            pltpu.SemaphoreType.DMA((7,)),
-            pltpu.SemaphoreType.DMA((2, 2)),
-            pltpu.SemaphoreType.DMA((2, 2)),
             pltpu.SemaphoreType.DMA((8,)),
-            pltpu.SemaphoreType.DMA((8,)),
+            pltpu.SemaphoreType.DMA((2, 3)),
+            pltpu.SemaphoreType.DMA((2, 3)),
+            pltpu.SemaphoreType.DMA((10,)),
+            pltpu.SemaphoreType.DMA((10,)),
             pltpu.SemaphoreType.DMA((2,)),
             pltpu.SemaphoreType.DMA((2,)),
             pltpu.SemaphoreType.DMA((3,)),
             pltpu.SemaphoreType.DMA((3,)),
+            pltpu.SemaphoreType.REGULAR((8,)),
         ],
         compiler_params=pltpu.CompilerParams(collective_id=0, has_side_effects=True, vmem_limit_bytes=40 << 20),
-    )(target, state.reshape(LM * 3 * ROWS, COLS), depth, obs_cells, obs_weights, obs_values, obs_precision)
+    )(
+        *(
+            pltpu.with_memory_space_constraint(a, pltpu.HBM)
+            for a in (
+                owner_map.reshape(-1), state.reshape(LM * 3 * ROWS, COLS), depth,
+                obs_cells, obs_weights, obs_values, obs_precision,
+            )
+        )
+    )
     vmem = pl.BlockSpec(memory_space=pltpu.VMEM)
     out = pl.pallas_call(
         combine_kernel,

time: 98.8 us -> 82.6 us (0.84)
  Pallas kernels: 91.6 us -> 82.5 us
  local copies, waits for them, and re-layouts: 5.46 us -> 0 us
  other arithmetic: 1.48 us -> 0 us
    pallas_call x1, Pallas kernels: 77.6 us -> 68.5 us  [local(): pl.pallas_call(main_kernel, name='forecast_and_reduce', out_shape=(jax.Sh...]
    unnamed x12 -> x0, local copies, waits for them, and re-layouts: 5.46 us -> none
where the time goes in v2:
time: 82.6 us; the launch traced here: 82.5 us
  Pallas kernels  82.5 us (100%)
    pallas_call x1, Pallas kernels, local(): pl.pallas_call(main_kernel, name='forecast_and_reduce', out_shape=(jax.Sh...  68.5 us
    pallas_call x1, Pallas kernels, local(): pl.pallas_call(combine_kernel, name='combine_members', out_shape=jax.Shap...  14 us

profile of v2, /device:TPU:1, one launch (start us, length us, event | category | flops | bytes accessed | tf_op | source)
XLA Modules:
  0.0 82.5 jit_solution(2731695271337156762)
XLA Ops:
  0.0 68.5 %forecast_and_reduce.1 = (f32[4,3,16,16,256]{4,3,2,1,0:T(8,128)S(1)}, f32[64,128]{1,0:T(8,128)S(1)}) custom-call(s32[64]{0:T(128)} %bitcast.4, f32[768,256]{1,0:T(8,128)} %bitcast.3, f32[16,256]{1,0:T(8,128)} %depth.1, s32[4,64,128]{2,1,0:T(8,128)} %cells_hbm.1, f32[4,64,128]{2,1,0:T(8,128)} %weights_hbm.1, f32[1,128,2,128]{3,2,1,0:T(2,128)} %values.1, ...), custom_call_target="tpu_custom_call" | custom-call | tf_op jit(solution)/shard_map/forecast_and_reduce/pallas_call | solution.py:438
  68.5 14.0 %combine_members.1 = f32[768,256]{1,0:T(8,128)} custom-call(f32[64,128]{1,0:T(8,128)S(1)} %get-tuple-element.7.total, f32[4,3,16,16,256]{4,3,2,1,0:T(8,128)S(1)} %get-tuple-element.8.fc), custom_call_target="tpu_custom_call" | custom-call | tf_op jit(solution)/shard_map/combine_members/pallas_call | solution.py:493

commit v3 on v2

--- a/solution.py
+++ b/solution.py
@@ -73,8 +73,8 @@
         packed[yb, r] = (q[0:8] << 16) | (q[8:16] & 0xFFFF)
 
 
-def interpolate(blocks, packed, inverse, cells, weights, pred):
-    for half in range(2):
+def interpolate(halves, blocks, packed, inverse, cells, weights, pred):
+    for half in halves:
 
         @pl.loop(0, BLK)
         def _(b):
@@ -100,9 +100,15 @@
                 pred[yb, b] = part if half == 0 else pred[yb, b] + part
 
 
+def tree_sum(terms):
+    while len(terms) > 1:
+        terms = [sum(terms[i : i + 2][1:], terms[i]) for i in range(0, len(terms), 2)]
+    return terms[0]
+
+
 def main_kernel(
     owners_hbm, state, depth, cells_hbm, weights_hbm, values, precisions, fc, total,
-    owners, target, st, dp, cells, weights, S, DB, H1, U1, V1, H2, packed, inverse, pred, X, tab_v, tab_p, Gs, rs, zs, zb, ga,
+    owners, target, st, dp, cells, weights, S, DB, H1, U1, V1, H2, packed, inverse, pred, X, sent, tab, Gs, rs, zs, zb, ga,
     load_sem, halo_send, halo_recv, ag_send, ag_recv, tab_send, tab_recv, red_send, red_recv, round_sem,
 ):
     s = lax.axis_index("space")
@@ -114,9 +120,6 @@
     place = (x * NM + y) * 2 + core
     left, right = (s + NS - 1) % NS, (s + 1) % NS
 
-    def member_of(q):
-        return ((q // 8) * (2 * NZ) + z * 2 + q % 2, (q // 2) % NM)
-
     def along_z(step):
         return (x * (2 * NZ) + ((z + step + NZ) % NZ) * 2 + core, y)
 
@@ -127,6 +130,20 @@
         return (s, (y + step + NM) % NM)
 
     partner = (s + 1 - 2 * core, y)
+
+    def beside(dx, dy, dc):
+        nx, ny, nc = (x + dx) % 4, (y + dy) % NM, core + dc - 2 * dc * core
+        return (nx * NM + ny) * 2 + nc, (nx * (2 * NZ) + z * 2 + nc, ny)
+
+    def hops(k, size):
+        return min(k, size - k)
+
+    steps = sorted(
+        ((dx, dy, dc) for dx in range(4) for dy in range(NM) for dc in range(2) if (dx, dy, dc) != (0, 0, 0)),
+        key=lambda d: -(hops(d[0], 4) + hops(d[1], NM)),
+    )
+    members = [beside(*step) for step in steps]
+    ring = [along_z(k) for k in sorted(range(1, NZ), key=lambda k: -hops(k, NZ))]
     own_rows = pl.ds(pl.multiple_of(y * BLK, BLK), BLK)
     loads = [
         pltpu.make_async_copy(state.at[:, pl.ds(0, OBS)], st.at[0], load_sem.at[0]),
@@ -135,6 +152,8 @@
         pltpu.make_async_copy(cells_hbm.at[:, own_rows], cells, load_sem.at[3]),
         pltpu.make_async_copy(weights_hbm.at[:, own_rows], weights, load_sem.at[4]),
         pltpu.make_async_copy(owners_hbm, owners, load_sem.at[5]),
+        pltpu.make_async_copy(values.at[0], sent.at[:, 0], load_sem.at[6]),
+        pltpu.make_async_copy(precisions.at[0], sent.at[:, 1], load_sem.at[7]),
     ]
     for load in loads:
         load.start()
@@ -163,6 +182,7 @@
     def hear(n):
         pl.semaphore_wait(round_sem.at[n], len(rounds[n]))
 
+    X[M : 2 * M] = jnp.zeros((M, BLK * OBS), jnp.float32)
     for load in loads[:3]:
         load.wait()
     for f in range(3):
@@ -202,9 +222,20 @@
     hear(1)
     tell(2)
 
+    loads[5].wait()
+
     @pl.loop(HALO + 3, HALO + ROWS - 3, unroll=2)
     def _(i):
         second_height(i, 1.0, DB, H1, U1, V1, H2)
+
+    @pl.loop(0, BLK)
+    def _(b):
+        me = y * BLK + b
+        owner = owners[me]
+        slot = jnp.int32(0)
+        for other in range(8192 // NS):
+            slot = slot + jnp.where((owners[other] == owner) & (other < me), 1, 0)
+        target[b] = owner * 2 + slot
 
     hear(2)
     tell(3)
@@ -252,25 +283,23 @@
 
     hear(5)
     tell(6)
-    own_v = pltpu.make_async_copy(values.at[0, s], tab_v.at[s], load_sem.at[6])
-    own_p = pltpu.make_async_copy(precisions.at[0, s], tab_p.at[s], load_sem.at[7])
-    own_v.start()
-    own_p.start()
+    loads[6].wait()
+    loads[7].wait()
+    tab[s] = sent[s]
 
     @pl.loop(1, NS)
     def _(i):
-        peer = (s + i) % NS
-        for k, (src, tab) in enumerate(((values, tab_v), (precisions, tab_p))):
-            pltpu.make_async_remote_copy(
-                src_ref=src.at[0, peer], dst_ref=tab.at[s], send_sem=tab_send.at[k], recv_sem=tab_recv.at[k],
-                device_id=(peer, y), device_id_type=MESH,
-            ).start()
+        peer = s + i
+        peer = peer - jnp.where(peer >= NS, NS, 0)
+        pltpu.make_async_remote_copy(
+            src_ref=sent.at[peer], dst_ref=tab.at[s], send_sem=tab_send, recv_sem=tab_recv,
+            device_id=(peer, y), device_id_type=MESH,
+        ).start()
 
     loads[3].wait()
     loads[4].wait()
-    loads[5].wait()
     pack_block(y, fc, packed, inverse)
-    interpolate([y], packed, inverse, cells, weights, pred)
+    interpolate([0], [y], packed, inverse, cells, weights, pred)
     hear(6)
     tell(7)
     up_first.wait_recv()
@@ -286,16 +315,7 @@
 
     up_w = share(fc.at[y, pl.ds(1, 2)], fc.at[y, pl.ds(1, 2)], 6, y_high)
     down_w = share(fc.at[y, pl.ds(1, 2)], fc.at[y, pl.ds(1, 2)], 7, y_low)
-
-    @pl.loop(0, BLK)
-    def _(b):
-        me = y * BLK + b
-        owner = owners[me]
-        slot = jnp.int32(0)
-        for other in range(8192 // NS):
-            slot = slot + jnp.where((owners[other] == owner) & (other < me), 1, 0)
-        target[b] = owner * 2 + slot
-
+    interpolate([1], [y], packed, inverse, cells, weights, pred)
     up_last.wait_recv()
     down_last.wait_recv()
     pack_block(y_low, fc, packed, inverse)
@@ -303,27 +323,21 @@
     pass_up.wait_recv()
     pass_down.wait_recv()
     pack_block(y_far, fc, packed, inverse)
-    interpolate([y_low, y_high, y_far], packed, inverse, cells, weights, pred)
+    interpolate([0, 1], [y_low, y_high, y_far], packed, inverse, cells, weights, pred)
     up_w.wait_recv()
     down_w.wait_recv()
     pass_u = share(fc.at[y_low, 1], fc.at[y_low, 1], 8, y_high)
     pass_v = share(fc.at[y_high, 2], fc.at[y_high, 2], 9, y_low)
     hear(7)
 
-    own_v.wait()
-    own_p.wait()
-    for k, tab in enumerate((tab_v, tab_p)):
-        everyone = tab.at[pl.ds(0, NS - 1)]
-        pltpu.make_async_copy(everyone, everyone, tab_recv.at[k]).wait()
-
+    everyone = tab.at[pl.ds(0, NS - 1)]
+    pltpu.make_async_copy(everyone, everyone, tab_recv).wait()
     scale = math.sqrt((M - 1) / N_OBS)
-    X[M : 2 * M] = jnp.zeros((M, BLK * OBS), jnp.float32)
-
     @pl.loop(0, BLK)
     def _(b):
         t = target[b]
-        seen = tab_v[t // 2, pl.ds(t % 2, 1), :]
-        factor = tab_p[t // 2, pl.ds(t % 2, 1), :] * scale
+        seen = tab[t // 2, 0, pl.ds(t % 2, 1), :]
+        factor = tab[t // 2, 1, pl.ds(t % 2, 1), :] * scale
         parts = [pred[yb, b] for yb in range(NM)]
         middle = jnp.sum(parts[0] + parts[1] + parts[2] + parts[3], axis=0, keepdims=True) * (1.0 / M)
         at = pl.ds(pl.multiple_of(b * OBS, OBS), OBS)
@@ -336,45 +350,31 @@
     )
     for q in range(GROUP):
         Gs[q] = gram[2 * q : 2 * q + 2]
-
-    @pl.loop(1, GROUP)
-    def _(i):
-        q = (place + i) % GROUP
+    for q, peer in members:
         pltpu.make_async_remote_copy(
             src_ref=Gs.at[q], dst_ref=rs.at[place], send_sem=red_send.at[0], recv_sem=red_recv.at[0],
-            device_id=member_of(q), device_id_type=MESH,
+            device_id=peer, device_id_type=MESH,
         ).start()
 
     rs[place] = Gs[place]
     others = rs.at[pl.ds(0, GROUP - 1)]
     pltpu.make_async_copy(others, others, red_recv.at[0]).wait()
-    mine = rs[0]
-    for q in range(1, GROUP):
-        mine = mine + rs[q]
+    mine = tree_sum([rs[q] for q in range(GROUP)])
     zs[...] = mine
     zb[z] = mine
-
-    @pl.loop(1, NZ)
-    def _(i):
-        other = (z + i) % NZ
+    for peer in ring:
         pltpu.make_async_remote_copy(
             src_ref=zs, dst_ref=zb.at[z], send_sem=red_send.at[1], recv_sem=red_recv.at[1],
-            device_id=(x * (2 * NZ) + other * 2 + core, y), device_id_type=MESH,
+            device_id=peer, device_id_type=MESH,
         ).start()
 
     others_z = zb.at[pl.ds(0, NZ - 1)]
     pltpu.make_async_copy(others_z, others_z, red_recv.at[1]).wait()
-    mine = zb[0]
-    for q in range(1, NZ):
-        mine = mine + zb[q]
-    ga[place] = mine
-
-    @pl.loop(1, GROUP)
-    def _(i):
-        q = (place + i) % GROUP
+    ga[place] = tree_sum([zb[q] for q in range(NZ)])
+    for q, peer in members:
         pltpu.make_async_remote_copy(
             src_ref=ga.at[place], dst_ref=ga.at[place], send_sem=red_send.at[2], recv_sem=red_recv.at[2],
-            device_id=member_of(q), device_id_type=MESH,
+            device_id=peer, device_id_type=MESH,
         ).start()
 
     pltpu.make_async_copy(others, others, red_send.at[0]).wait()
@@ -388,40 +388,72 @@
     pass_v.wait_recv()
     for copy in (up_first, down_first, up_last, down_last, pass_up, pass_down, up_w, down_w, pass_u, pass_v):
         copy.wait_send()
-    for k, tab in enumerate((tab_v, tab_p)):
-        everyone = tab.at[pl.ds(0, NS - 1)]
-        pltpu.make_async_copy(everyone, everyone, tab_send.at[k]).wait()
+    pltpu.make_async_copy(everyone, everyone, tab_send).wait()
+
+
+def inverse_factor(g):
+    sub = lax.broadcasted_iota(jnp.int32, (8, 2 * M), 0)
+    lane = lax.broadcasted_iota(jnp.int32, (8, 2 * M), 1)
+    work = []
+    for n in range(M // 8):
+        diagonal = jnp.where(lane == sub + 8 * n, float(M - 1), 0.0)
+        right = jnp.where(lane == sub + 8 * n + M, 1.0, 0.0)
+        work.append(jnp.where(lane < M, g[8 * n : 8 * n + 8] + diagonal, right))
+
+    def spread(row):
+        return jnp.broadcast_to(row, (8, 2 * M))
+
+    result = []
+    for n in range(M // 8):
+        below = range(n, M // 8)
+        column = [{r: spread(work[r][:, 8 * n + j : 8 * n + j + 1]) for r in below} for j in range(8)]
+        pivots = jnp.zeros((8, 2 * M), jnp.float32)
+        for j in range(8):
+            pivot = spread(column[j][n][j : j + 1])
+            pivots = jnp.where(sub == j, pivot, pivots)
+            inverse = 1.0 / pivot
+            ratio = {r: column[j][r] * inverse for r in below}
+            ratio[n] = jnp.where(sub > j, ratio[n], 0.0)
+            for k in range(j + 1, 8):
+                head = spread(column[k][n][j : j + 1])
+                for r in below:
+                    column[k][r] = column[k][r] - ratio[r] * head
+            row = spread(work[n][j : j + 1])
+            for r in below:
+                work[r] = work[r] - ratio[r] * row
+        result.append(jnp.where(lane >= M, work[n] * (1.0 / jnp.sqrt(pivots)), 0.0))
+    return jnp.concatenate(result, axis=0)
+
+
+def two_terms(value):
+    high = value.astype(jnp.bfloat16)
+    return high, (value - high.astype(jnp.float32)).astype(jnp.bfloat16)
 
 
 def combine_kernel(total, fc, out, inv_ref, held, sem):
     y = lax.axis_index("mem")
     g = total[...]
+    lower_inv = inverse_factor(g)
+    inv_ref[...] = lower_inv
     row = lax.broadcasted_iota(jnp.int32, (M, 2 * M), 0)
     lane = lax.broadcasted_iota(jnp.int32, (M, 2 * M), 1)
-    proj = g[:, M : M + 1]
-    eye = jnp.where(lane == row + M, 1.0, 0.0)
-    work = jnp.where(lane < M, g + jnp.where(lane == row, float(M - 1), 0.0), eye)
-    for k in range(M - 1):
-        pivot = work[k : k + 1, :]
-        ratio = work[:, k : k + 1] * (1.0 / work[k : k + 1, k : k + 1])
-        work = work - jnp.where(row > k, ratio * pivot, 0.0)
-    diagonal = jnp.sum(jnp.where(lane == row, work, 0.0), axis=1, keepdims=True)
-    lower_inv = work[:, M:] * (1.0 / jnp.sqrt(diagonal))
-    inv_ref[...] = lower_inv
-    square = jnp.where(row[:, :M] == lane[:, :M], 1.0, 0.0)
-    proj_row = jnp.broadcast_to(jnp.sum(square * proj, axis=0, keepdims=True), (8, M))
+    square = jnp.where(lane == row + M, jnp.broadcast_to(g[:, M : M + 1], (M, 2 * M)), 0.0)
+    proj_row = jnp.broadcast_to(jnp.sum(square, axis=0, keepdims=True), (8, 2 * M))
     first = lax.dot_general(
         proj_row, lower_inv, (((1,), (1,)), ((), ())), precision=HIGHEST, preferred_element_type=jnp.float32
     )
     mean_weights = jnp.dot(first, lower_inv, precision=HIGHEST, preferred_element_type=jnp.float32)[0:1]
     coef = mean_weights + math.sqrt(M - 1) * inv_ref[pl.ds(pl.multiple_of(y * LM, LM), LM), :]
-    mixing = coef + (1.0 - jnp.sum(coef, axis=1, keepdims=True)) * (1.0 / M)
+    mixing = (coef + (1.0 - jnp.sum(coef, axis=1, keepdims=True)) * (1.0 / M))[:, M:]
+    mix_high, mix_low = two_terms(mixing)
+    mix = jnp.concatenate([mix_high, mix_high, mix_low], axis=1)
     for f in range(3):
 
-        @pl.loop(0, ROWS)
+        @pl.loop(0, ROWS, unroll=ROWS)
         def _(r):
-            prior = jnp.concatenate([fc[yb, f, r] for yb in range(NM)], axis=0)
-            new = jnp.dot(mixing, prior, precision=HIGHEST, preferred_element_type=jnp.float32)
+            high, low = two_terms(jnp.concatenate([fc[yb, f, r] for yb in range(NM)], axis=0))
+            prior = jnp.concatenate([high, low, high], axis=0)
+            new = jnp.dot(mix, prior, preferred_element_type=jnp.float32)
             for c in range(2):
                 held[c, pl.ds(f * ROWS + r, LM, stride=3 * ROWS), :] = new[:, c * OBS : (c + 1) * OBS]
 
@@ -461,8 +493,8 @@
             pltpu.VMEM((NM, LM, OBS), f32),
             pltpu.VMEM((NM, BLK, LM, OBS), f32),
             pltpu.VMEM((2 * M, BLK * OBS), f32),
-            pltpu.VMEM((NS, 2, OBS), f32),
-            pltpu.VMEM((NS, 2, OBS), f32),
+            pltpu.VMEM((NS, 2, 2, OBS), f32),
+            pltpu.VMEM((NS, 2, 2, OBS), f32),
             pltpu.VMEM((GROUP, 2, 2 * M), f32),
             pltpu.VMEM((GROUP, 2, 2 * M), f32),
             pltpu.VMEM((2, 2 * M), f32),
@@ -473,8 +505,8 @@
             pltpu.SemaphoreType.DMA((2, 3)),
             pltpu.SemaphoreType.DMA((10,)),
             pltpu.SemaphoreType.DMA((10,)),
-            pltpu.SemaphoreType.DMA((2,)),
-            pltpu.SemaphoreType.DMA((2,)),
+            pltpu.SemaphoreType.DMA,
+            pltpu.SemaphoreType.DMA,
             pltpu.SemaphoreType.DMA((3,)),
             pltpu.SemaphoreType.DMA((3,)),
             pltpu.SemaphoreType.REGULAR((8,)),
@@ -497,7 +529,7 @@
         in_specs=[vmem, vmem],
         out_specs=any_space,
         scratch_shapes=[
-            pltpu.VMEM((M, M), f32),
+            pltpu.VMEM((M, 2 * M), f32),
             pltpu.VMEM((2, LM * 3 * ROWS, OBS), f32),
             pltpu.SemaphoreType.DMA((2,)),
         ],

time: 82.6 us -> 68.8 us (0.83)
  Pallas kernels: 82.5 us -> 68.6 us
    pallas_call x1, Pallas kernels: 14 us -> 3.9 us  [local(): pl.pallas_call(combine_kernel, name='combine_members', out_shape=jax.Shap...]
    pallas_call x1, Pallas kernels: 68.5 us -> 64.7 us  [local(): pl.pallas_call(main_kernel, name='forecast_and_reduce', out_shape=(jax.Sh...]
where the time goes in v3:
time: 68.8 us; the launch traced here: 68.6 us
  Pallas kernels  68.6 us (100%)
    pallas_call x1, Pallas kernels, local(): pl.pallas_call(main_kernel, name='forecast_and_reduce', out_shape=(jax.Sh...  64.7 us
    pallas_call x1, Pallas kernels, local(): pl.pallas_call(combine_kernel, name='combine_members', out_shape=jax.Shap...  3.9 us

profile of v3, /device:TPU:1, one launch (start us, length us, event | category | flops | bytes accessed | tf_op | source)
XLA Modules:
  0.0 68.6 jit_solution(2742597188236912357)
XLA Ops:
  0.0 64.7 %forecast_and_reduce.1 = (f32[4,3,16,16,256]{4,3,2,1,0:T(8,128)S(1)}, f32[64,128]{1,0:T(8,128)S(1)}) custom-call(s32[64]{0:T(128)} %bitcast.4, f32[768,256]{1,0:T(8,128)} %bitcast.3, f32[16,256]{1,0:T(8,128)} %depth.1, s32[4,64,128]{2,1,0:T(8,128)} %cells_hbm.1, f32[4,64,128]{2,1,0:T(8,128)} %weights_hbm.1, f32[1,128,2,128]{3,2,1,0:T(2,128)} %values.1, ...), custom_call_target="tpu_custom_call" | custom-call | tf_op jit(solution)/shard_map/forecast_and_reduce/pallas_call | solution.py:470
  64.7 3.9 %combine_members.1 = f32[768,256]{1,0:T(8,128)} custom-call(f32[64,128]{1,0:T(8,128)S(1)} %get-tuple-element.7.total, f32[4,3,16,16,256]{4,3,2,1,0:T(8,128)S(1)} %get-tuple-element.8.fc), custom_call_target="tpu_custom_call" | custom-call | tf_op jit(solution)/shard_map/combine_members/pallas_call | solution.py:525

commit v4 on v3

--- a/solution.py
+++ b/solution.py
@@ -24,7 +24,6 @@
 EAST, HEIGHT, NORTH = 0, 1, 2
 FIELD = (HEIGHT, EAST, NORTH)
 MESH = pl.DeviceIdType.MESH
-HIGHEST = lax.Precision.HIGHEST
 mass_rate = 0.2
 wave_rate = 0.2
 turn_rate = 0.1
@@ -59,45 +58,48 @@
         H2[i, g] = (H1[i, g] - mass_rate * change) * keep
 
 
-def pack_block(yb, fc, packed, inverse):
+def pack_block(yb, height, packed, inverse):
     top = lax.fori_loop(
-        0, ROWS, lambda r, t: jnp.maximum(t, jnp.abs(fc[yb, 0, r])), jnp.zeros((LM, COLS), jnp.float32)
+        0, ROWS, lambda r, t: jnp.maximum(t, jnp.abs(height(r))), jnp.zeros((LM, COLS), jnp.float32), unroll=4
     )
     top = jnp.maximum(jnp.max(top, axis=1, keepdims=True), 1e-30)
     scale = 32000.0 / top
     inverse[yb] = jnp.broadcast_to(top * (1.0 / 32000.0), (LM, OBS))
 
-    @pl.loop(0, ROWS)
+    @pl.loop(0, ROWS, unroll=4)
     def _(r):
-        q = jnp.floor(fc[yb, 0, r] * scale + 0.5).astype(jnp.int32)
+        q = jnp.floor(height(r) * scale + 0.5).astype(jnp.int32)
         packed[yb, r] = (q[0:8] << 16) | (q[8:16] & 0xFFFF)
 
 
-def interpolate(halves, blocks, packed, inverse, cells, weights, pred):
-    for half in halves:
-
-        @pl.loop(0, BLK)
-        def _(b):
-            lane, chunk, weight = [], [], []
-            for k in range(2):
-                cell = jnp.broadcast_to(cells[half * 2 + k, pl.ds(b, 1), :], (8, OBS))
-                lane.append(cell & (OBS - 1))
-                chunk.append(cell >> 7)
-                weight.append(jnp.broadcast_to(weights[half * 2 + k, pl.ds(b, 1), :], (8, OBS)))
-            held = [[jnp.zeros((8, OBS), jnp.int32) for _ in blocks] for _ in range(2)]
-            for c in range(ROWS * COLS // OBS):
-                row, col = c // 2, (c % 2) * OBS
-                here = [chunk[k] == c for k in range(2)]
-                for g, yb in enumerate(blocks):
-                    values = packed[yb, row, :, col : col + OBS]
-                    for k in range(2):
-                        found = jnp.take_along_axis(values, lane[k], axis=1, mode="promise_in_bounds")
-                        held[k][g] = jnp.where(here[k], found, held[k][g])
+def interpolate(half, span, blocks, packed, inverse, cells, weights, pred):
+    @pl.loop(*span)
+    def _(b):
+        lane, chunk, weight = [], [], []
+        for k in range(2):
+            cell = jnp.broadcast_to(cells[half * 2 + k, pl.ds(b, 1), :], (8, OBS))
+            lane.append(cell & (OBS - 1))
+            chunk.append(cell >> 7)
+            weight.append(jnp.broadcast_to(weights[half * 2 + k, pl.ds(b, 1), :], (8, OBS)))
+        held = [[jnp.zeros((8, OBS), jnp.int32) for _ in blocks] for _ in range(2)]
+        for c in range(ROWS * COLS // OBS):
+            row, col = c // 2, (c % 2) * OBS
+            here = [chunk[k] == c for k in range(2)]
             for g, yb in enumerate(blocks):
-                high = sum((held[k][g] >> 16).astype(jnp.float32) * weight[k] for k in range(2))
-                low = sum(((held[k][g] << 16) >> 16).astype(jnp.float32) * weight[k] for k in range(2))
-                part = jnp.concatenate([high, low], axis=0) * inverse[yb]
-                pred[yb, b] = part if half == 0 else pred[yb, b] + part
+                values = packed[yb, row, :, col : col + OBS]
+                for k in range(2):
+                    found = jnp.take_along_axis(values, lane[k], axis=1, mode="promise_in_bounds")
+                    held[k][g] = jnp.where(here[k], found, held[k][g])
+        for g, yb in enumerate(blocks):
+            high = sum((held[k][g] >> 16).astype(jnp.float32) * weight[k] for k in range(2))
+            low = sum(((held[k][g] << 16) >> 16).astype(jnp.float32) * weight[k] for k in range(2))
+            part = jnp.concatenate([high, low], axis=0) * inverse[yb]
+            pred[yb, b] = part if half == 0 else pred[yb, b] + part
+
+
+def two_terms(value):
+    high = value.astype(jnp.bfloat16)
+    return high, (value - high.astype(jnp.float32)).astype(jnp.bfloat16)
 
 
 def tree_sum(terms):
@@ -108,8 +110,8 @@
 
 def main_kernel(
     owners_hbm, state, depth, cells_hbm, weights_hbm, values, precisions, fc, total,
-    owners, target, st, dp, cells, weights, S, DB, H1, U1, V1, H2, packed, inverse, pred, X, sent, tab, Gs, rs, zs, zb, ga,
-    load_sem, halo_send, halo_recv, ag_send, ag_recv, tab_send, tab_recv, red_send, red_recv, round_sem,
+    owners, st, dp, cells, weights, S, DB, H1, U1, V1, H2, packed, inverse, pred, XH, XL, sent, tab, picked, given, Gs, rs, zs, zb, ga,
+    load_sem, halo_send, halo_recv, ag_send, ag_recv, tab_send, tab_recv, red_send, red_recv, round_sem, pick_send, pick_recv,
 ):
     s = lax.axis_index("space")
     y = lax.axis_index("mem")
@@ -182,7 +184,8 @@
     def hear(n):
         pl.semaphore_wait(round_sem.at[n], len(rounds[n]))
 
-    X[M : 2 * M] = jnp.zeros((M, BLK * OBS), jnp.float32)
+    for terms in (XH, XL):
+        terms[M : 2 * M] = jnp.zeros((M, BLK * OBS), jnp.bfloat16)
     for load in loads[:3]:
         load.wait()
     for f in range(3):
@@ -212,35 +215,19 @@
     def _(i):
         height_step(i, 1.0, S, DB, H1)
 
-    hear(0)
-    tell(1)
-
     @pl.loop(HALO + 2, HALO + ROWS - 2, unroll=2)
     def _(i):
         wind_step(i, S, H1, U1, V1)
 
-    hear(1)
-    tell(2)
-
-    loads[5].wait()
+    hear(0)
+    tell(1)
 
     @pl.loop(HALO + 3, HALO + ROWS - 3, unroll=2)
     def _(i):
         second_height(i, 1.0, DB, H1, U1, V1, H2)
 
-    @pl.loop(0, BLK)
-    def _(b):
-        me = y * BLK + b
-        owner = owners[me]
-        slot = jnp.int32(0)
-        for other in range(8192 // NS):
-            slot = slot + jnp.where((owners[other] == owner) & (other < me), 1, 0)
-        target[b] = owner * 2 + slot
-
-    hear(2)
-    tell(3)
     for halo in halos:
-        halo.wait()
+        halo.wait_recv()
 
     inside_low = jnp.where(s > 0, 1.0, 0.0).astype(jnp.float32)
     inside_high = jnp.where(s < NS - 1, 1.0, 0.0).astype(jnp.float32)
@@ -250,13 +237,11 @@
     for i in range(1, 5):
         height_step(i, inside_low if i < HALO else 1.0, S, DB, H1)
         height_step(EXT - 1 - i, inside_high if i < HALO else 1.0, S, DB, H1)
-    hear(3)
-    tell(4)
+    hear(1)
+    tell(2)
     for i in range(2, 6):
         wind_step(i, S, H1, U1, V1)
         wind_step(EXT - 1 - i, S, H1, U1, V1)
-    hear(4)
-    tell(5)
     for i in range(3, 7):
         second_height(i, inside_low if i < HALO else 1.0, DB, H1, U1, V1, H2)
         second_height(EXT - 1 - i, inside_high if i < HALO else 1.0, DB, H1, U1, V1, H2)
@@ -277,77 +262,129 @@
     up_last = share(sent_last, fc.at[y, 0, last], 2, y_high)
     down_last = share(sent_first, fc.at[y, 0, first], 3, y_low)
 
-    @pl.loop(0, ROWS, unroll=2)
-    def _(r):
-        fc[y, 0, r] = H2[HALO + r]
-
+    loads[3].wait()
+    loads[4].wait()
+    pack_block(y, lambda r: H2[HALO + r], packed, inverse)
+    interpolate(0, (0, BLK), [y], packed, inverse, cells, weights, pred)
+    hear(2)
+    tell(3)
+    interpolate(1, (0, BLK // 2), [y], packed, inverse, cells, weights, pred)
+    hear(3)
+    tell(4)
+    interpolate(1, (BLK // 2, BLK), [y], packed, inverse, cells, weights, pred)
+    up_first.wait_recv()
+    down_first.wait_recv()
+    pass_up = share(fc.at[y_low, 0, first], fc.at[y_low, 0, first], 4, y_high)
+    pass_down = share(fc.at[y_high, 0, last], fc.at[y_high, 0, last], 5, y_low)
+    hear(4)
+    tell(5)
+
+    @pl.loop(HALO, HALO + ROWS, unroll=2)
+    def _(i):
+        u, v, h = U1[i], V1[i], H2[i]
+        fc[y, 1, i - HALO] = u - wave_rate * (H2[i + 1] - H2[i - 1]) + turn_rate * v
+        fc[y, 2, i - HALO] = v - wave_rate * (east(h) - west(h)) - turn_rate * u
+
+    loads[6].wait()
+    loads[7].wait()
     hear(5)
     tell(6)
-    loads[6].wait()
-    loads[7].wait()
-    tab[s] = sent[s]
+
+    kind, slot = y // 2, y % 2
+
+    def row_for(peer):
+        return sent.at[peer, kind, pl.ds(slot, 1)]
+
+    own_row = pltpu.make_async_copy(row_for(s), tab.at[s], load_sem.at[8])
+    own_row.start()
 
     @pl.loop(1, NS)
     def _(i):
         peer = s + i
         peer = peer - jnp.where(peer >= NS, NS, 0)
         pltpu.make_async_remote_copy(
-            src_ref=sent.at[peer], dst_ref=tab.at[s], send_sem=tab_send, recv_sem=tab_recv,
+            src_ref=row_for(peer), dst_ref=tab.at[s], send_sem=tab_send, recv_sem=tab_recv,
             device_id=(peer, y), device_id_type=MESH,
         ).start()
 
-    loads[3].wait()
-    loads[4].wait()
-    pack_block(y, fc, packed, inverse)
-    interpolate([0], [y], packed, inverse, cells, weights, pred)
+    up_last.wait_recv()
+    down_last.wait_recv()
+    pack_block(y_low, lambda r: fc[y_low, 0, r], packed, inverse)
+    pack_block(y_high, lambda r: fc[y_high, 0, r], packed, inverse)
     hear(6)
     tell(7)
-    up_first.wait_recv()
-    down_first.wait_recv()
-    pass_up = share(fc.at[y_low, 0, first], fc.at[y_low, 0, first], 4, y_high)
-    pass_down = share(fc.at[y_high, 0, last], fc.at[y_high, 0, last], 5, y_low)
-
-    @pl.loop(HALO, HALO + ROWS, unroll=2)
-    def _(i):
-        u, v, h = U1[i], V1[i], H2[i]
-        fc[y, 1, i - HALO] = u - wave_rate * (H2[i + 1] - H2[i - 1]) + turn_rate * v
-        fc[y, 2, i - HALO] = v - wave_rate * (east(h) - west(h)) - turn_rate * u
-
-    up_w = share(fc.at[y, pl.ds(1, 2)], fc.at[y, pl.ds(1, 2)], 6, y_high)
-    down_w = share(fc.at[y, pl.ds(1, 2)], fc.at[y, pl.ds(1, 2)], 7, y_low)
-    interpolate([1], [y], packed, inverse, cells, weights, pred)
-    up_last.wait_recv()
-    down_last.wait_recv()
-    pack_block(y_low, fc, packed, inverse)
-    pack_block(y_high, fc, packed, inverse)
     pass_up.wait_recv()
     pass_down.wait_recv()
-    pack_block(y_far, fc, packed, inverse)
-    interpolate([0, 1], [y_low, y_high, y_far], packed, inverse, cells, weights, pred)
-    up_w.wait_recv()
-    down_w.wait_recv()
-    pass_u = share(fc.at[y_low, 1], fc.at[y_low, 1], 8, y_high)
-    pass_v = share(fc.at[y_high, 2], fc.at[y_high, 2], 9, y_low)
-    hear(7)
-
+    up_u = share(fc.at[y, 1], fc.at[y, 1], 6, y_high)
+    down_u = share(fc.at[y, 1], fc.at[y, 1], 7, y_low)
+    pack_block(y_far, lambda r: fc[y_far, 0, r], packed, inverse)
+    rest = [y_low, y_high, y_far]
+    interpolate(0, (0, BLK), rest, packed, inverse, cells, weights, pred)
+    interpolate(1, (0, BLK // 2), rest, packed, inverse, cells, weights, pred)
+
+    loads[5].wait()
+    blocks = 8192 // NS
+    across = jnp.broadcast_to(owners[...], (blocks, blocks))
+    down_at = lax.broadcasted_iota(jnp.int32, (blocks, blocks), 0)
+    across_at = lax.broadcasted_iota(jnp.int32, (blocks, blocks), 1)
+    mine_down = jnp.sum(jnp.where(down_at == across_at, across, 0), axis=1, keepdims=True)
+    earlier = jnp.where((across == mine_down) & (across_at < down_at), 1, 0)
+    slot_down = jnp.sum(earlier, axis=1, keepdims=True)
+    wanted = jnp.where(slot_down == slot, mine_down, -1)
+    choose = jnp.where(lax.broadcasted_iota(jnp.int32, (blocks, NS), 1) == wanted, 1.0, 0.0).astype(jnp.bfloat16)
+    own_row.wait()
     everyone = tab.at[pl.ds(0, NS - 1)]
     pltpu.make_async_copy(everyone, everyone, tab_recv).wait()
+    rows = tab[...].reshape(NS, OBS)
+    high, low = two_terms(rows)
+    left_over = (rows - high.astype(jnp.float32) - low.astype(jnp.float32)).astype(jnp.bfloat16)
+
+    def take(term):
+        return jnp.dot(choose, term, preferred_element_type=jnp.float32)
+
+    chosen = take(high) + (take(low) + take(left_over))
+    for q in range(NM):
+        picked[q] = chosen[q * BLK : (q + 1) * BLK]
+    hand = []
+    for step in range(1, NM):
+        peer = (y + step) % NM
+        hand.append(
+            pltpu.make_async_remote_copy(
+                src_ref=picked.at[peer], dst_ref=given.at[y], send_sem=pick_send.at[step], recv_sem=pick_recv.at[step],
+                device_id=(s, peer), device_id_type=MESH,
+            )
+        )
+        hand[-1].start()
+    given[y] = picked[y]
+    up_v = share(fc.at[y, 2], fc.at[y, 2], 10, y_high)
+    down_v = share(fc.at[y, 2], fc.at[y, 2], 11, y_low)
+    interpolate(1, (BLK // 2, BLK), rest, packed, inverse, cells, weights, pred)
+    hear(7)
+    for copy in hand:
+        copy.wait_recv()
+
     scale = math.sqrt((M - 1) / N_OBS)
+
+    def keep_terms(rows, at, value):
+        XH[rows, at], XL[rows, at] = two_terms(value)
+
     @pl.loop(0, BLK)
     def _(b):
-        t = target[b]
-        seen = tab[t // 2, 0, pl.ds(t % 2, 1), :]
-        factor = tab[t // 2, 1, pl.ds(t % 2, 1), :] * scale
+        at_block = pl.ds(b, 1)
+        seen = given[0, at_block, :] + given[1, at_block, :]
+        factor = (given[2, at_block, :] + given[3, at_block, :]) * scale
         parts = [pred[yb, b] for yb in range(NM)]
         middle = jnp.sum(parts[0] + parts[1] + parts[2] + parts[3], axis=0, keepdims=True) * (1.0 / M)
         at = pl.ds(pl.multiple_of(b * OBS, OBS), OBS)
         for yb in range(NM):
-            X[yb * LM : (yb + 1) * LM, at] = (parts[yb] - middle) * factor
-        X[M : M + 1, at] = (seen - middle) * factor
-
-    gram = lax.dot_general(
-        X[0:M], X[...], (((1,), (1,)), ((), ())), precision=HIGHEST, preferred_element_type=jnp.float32
-    )
+            keep_terms(slice(yb * LM, (yb + 1) * LM), at, (parts[yb] - middle) * factor)
+        depart = jnp.broadcast_to((seen - middle) * factor, (LM, OBS))
+        keep_terms(slice(M, M + LM), at, jnp.where(lax.broadcasted_iota(jnp.int32, (LM, OBS), 0) == 0, depart, 0.0))
+
+    def product(a, b):
+        return lax.dot_general(a[0:M], b[...], (((1,), (1,)), ((), ())), preferred_element_type=jnp.float32)
+
+    gram = product(XH, XH) + (product(XH, XL) + product(XL, XH))
     for q in range(GROUP):
         Gs[q] = gram[2 * q : 2 * q + 2]
     for q, peer in members:
@@ -357,8 +394,17 @@
         ).start()
 
     rs[place] = Gs[place]
+
+    @pl.loop(0, ROWS, unroll=2)
+    def _(r):
+        fc[y, 0, r] = H2[HALO + r]
+
     others = rs.at[pl.ds(0, GROUP - 1)]
     pltpu.make_async_copy(others, others, red_recv.at[0]).wait()
+    up_u.wait_recv()
+    down_u.wait_recv()
+    up_v.wait_recv()
+    down_v.wait_recv()
     mine = tree_sum([rs[q] for q in range(GROUP)])
     zs[...] = mine
     zb[z] = mine
@@ -368,6 +414,8 @@
             device_id=peer, device_id_type=MESH,
         ).start()
 
+    pass_u = share(fc.at[y_low, 1], fc.at[y_low, 1], 8, y_high)
+    pass_v = share(fc.at[y_high, 2], fc.at[y_high, 2], 9, y_low)
     others_z = zb.at[pl.ds(0, NZ - 1)]
     pltpu.make_async_copy(others_z, others_z, red_recv.at[1]).wait()
     ga[place] = tree_sum([zb[q] for q in range(NZ)])
@@ -386,7 +434,9 @@
         total[2 * q : 2 * q + 2] = ga[q]
     pass_u.wait_recv()
     pass_v.wait_recv()
-    for copy in (up_first, down_first, up_last, down_last, pass_up, pass_down, up_w, down_w, pass_u, pass_v):
+    for copy in halos + hand:
+        copy.wait_send()
+    for copy in (up_first, down_first, up_last, down_last, pass_up, pass_down, up_u, down_u, up_v, down_v, pass_u, pass_v):
         copy.wait_send()
     pltpu.make_async_copy(everyone, everyone, tab_send).wait()
 
@@ -400,12 +450,16 @@
         right = jnp.where(lane == sub + 8 * n + M, 1.0, 0.0)
         work.append(jnp.where(lane < M, g[8 * n : 8 * n + 8] + diagonal, right))
 
+    spot = lax.broadcasted_iota(jnp.int32, (M, 2 * M), 0) == lax.broadcasted_iota(jnp.int32, (M, 2 * M), 1)
+    proj = jnp.where(spot, jnp.broadcast_to(g[:, M : M + 1], (M, 2 * M)), 0.0)
+    work.append(jnp.broadcast_to(jnp.sum(proj, axis=0, keepdims=True), (8, 2 * M)))
+
     def spread(row):
         return jnp.broadcast_to(row, (8, 2 * M))
 
     result = []
     for n in range(M // 8):
-        below = range(n, M // 8)
+        below = range(n, M // 8 + 1)
         column = [{r: spread(work[r][:, 8 * n + j : 8 * n + j + 1]) for r in below} for j in range(8)]
         pivots = jnp.zeros((8, 2 * M), jnp.float32)
         for j in range(8):
@@ -422,29 +476,16 @@
             for r in below:
                 work[r] = work[r] - ratio[r] * row
         result.append(jnp.where(lane >= M, work[n] * (1.0 / jnp.sqrt(pivots)), 0.0))
-    return jnp.concatenate(result, axis=0)
-
-
-def two_terms(value):
-    high = value.astype(jnp.bfloat16)
-    return high, (value - high.astype(jnp.float32)).astype(jnp.bfloat16)
+    return jnp.concatenate(result, axis=0), -work[M // 8][0:1]
 
 
 def combine_kernel(total, fc, out, inv_ref, held, sem):
     y = lax.axis_index("mem")
-    g = total[...]
-    lower_inv = inverse_factor(g)
+    lower_inv, mean_weights = inverse_factor(total[...])
     inv_ref[...] = lower_inv
-    row = lax.broadcasted_iota(jnp.int32, (M, 2 * M), 0)
-    lane = lax.broadcasted_iota(jnp.int32, (M, 2 * M), 1)
-    square = jnp.where(lane == row + M, jnp.broadcast_to(g[:, M : M + 1], (M, 2 * M)), 0.0)
-    proj_row = jnp.broadcast_to(jnp.sum(square, axis=0, keepdims=True), (8, 2 * M))
-    first = lax.dot_general(
-        proj_row, lower_inv, (((1,), (1,)), ((), ())), precision=HIGHEST, preferred_element_type=jnp.float32
-    )
-    mean_weights = jnp.dot(first, lower_inv, precision=HIGHEST, preferred_element_type=jnp.float32)[0:1]
     coef = mean_weights + math.sqrt(M - 1) * inv_ref[pl.ds(pl.multiple_of(y * LM, LM), LM), :]
-    mixing = (coef + (1.0 - jnp.sum(coef, axis=1, keepdims=True)) * (1.0 / M))[:, M:]
+    coef = coef[:, M:]
+    mixing = coef + (1.0 - jnp.sum(coef, axis=1, keepdims=True)) * (1.0 / M)
     mix_high, mix_low = two_terms(mixing)
     mix = jnp.concatenate([mix_high, mix_high, mix_low], axis=1)
     for f in range(3):
@@ -477,8 +518,7 @@
         in_specs=[any_space] * 7,
         out_specs=(pl.BlockSpec(memory_space=pltpu.VMEM), pl.BlockSpec(memory_space=pltpu.VMEM)),
         scratch_shapes=[
-            pltpu.SMEM((8192 // NS,), jnp.int32),
-            pltpu.SMEM((BLK,), jnp.int32),
+            pltpu.VMEM((1, 8192 // NS), jnp.int32),
             pltpu.VMEM((2, LM * 3 * ROWS, OBS), f32),
             pltpu.VMEM((ROWS, COLS), f32),
             pltpu.VMEM((4, BLK, OBS), jnp.int32),
@@ -492,31 +532,36 @@
             pltpu.VMEM((NM, ROWS, 8, COLS), jnp.int32),
             pltpu.VMEM((NM, LM, OBS), f32),
             pltpu.VMEM((NM, BLK, LM, OBS), f32),
-            pltpu.VMEM((2 * M, BLK * OBS), f32),
+            pltpu.VMEM((2 * M, BLK * OBS), jnp.bfloat16),
+            pltpu.VMEM((2 * M, BLK * OBS), jnp.bfloat16),
             pltpu.VMEM((NS, 2, 2, OBS), f32),
-            pltpu.VMEM((NS, 2, 2, OBS), f32),
+            pltpu.VMEM((NS, 1, OBS), f32),
+            pltpu.VMEM((NM, BLK, OBS), f32),
+            pltpu.VMEM((NM, BLK, OBS), f32),
             pltpu.VMEM((GROUP, 2, 2 * M), f32),
             pltpu.VMEM((GROUP, 2, 2 * M), f32),
             pltpu.VMEM((2, 2 * M), f32),
             pltpu.VMEM((NZ, 2, 2 * M), f32),
             pltpu.VMEM((GROUP, 2, 2 * M), f32),
-            pltpu.SemaphoreType.DMA((8,)),
+            pltpu.SemaphoreType.DMA((9,)),
             pltpu.SemaphoreType.DMA((2, 3)),
             pltpu.SemaphoreType.DMA((2, 3)),
-            pltpu.SemaphoreType.DMA((10,)),
-            pltpu.SemaphoreType.DMA((10,)),
+            pltpu.SemaphoreType.DMA((12,)),
+            pltpu.SemaphoreType.DMA((12,)),
             pltpu.SemaphoreType.DMA,
             pltpu.SemaphoreType.DMA,
             pltpu.SemaphoreType.DMA((3,)),
             pltpu.SemaphoreType.DMA((3,)),
             pltpu.SemaphoreType.REGULAR((8,)),
+            pltpu.SemaphoreType.DMA((NM,)),
+            pltpu.SemaphoreType.DMA((NM,)),
         ],
         compiler_params=pltpu.CompilerParams(collective_id=0, has_side_effects=True, vmem_limit_bytes=40 << 20),
     )(
         *(
             pltpu.with_memory_space_constraint(a, pltpu.HBM)
             for a in (
-                owner_map.reshape(-1), state.reshape(LM * 3 * ROWS, COLS), depth,
+                owner_map.reshape(1, -1), state.reshape(LM * 3 * ROWS, COLS), depth,
                 obs_cells, obs_weights, obs_values, obs_precision,
             )
         )

time: 68.8 us -> 62.9 us (0.914)
  Pallas kernels: 68.6 us -> 62.8 us
    pallas_call x1, Pallas kernels: 64.7 us -> 59.1 us  [local(): pl.pallas_call(main_kernel, name='forecast_and_reduce', out_shape=(jax.Sh...]
where the time goes in v4:
time: 62.9 us; the launch traced here: 62.8 us
  Pallas kernels  62.8 us (100%)
    pallas_call x1, Pallas kernels, local(): pl.pallas_call(main_kernel, name='forecast_and_reduce', out_shape=(jax.Sh...  59.1 us
    pallas_call x1, Pallas kernels, local(): pl.pallas_call(combine_kernel, name='combine_members', out_shape=jax.Shap...  3.68 us

profile of v4, /device:TPU:1, one launch (start us, length us, event | category | flops | bytes accessed | tf_op | source)
XLA Modules:
  0.0 62.8 jit_solution(12338727898638038773)
XLA Ops:
  0.0 59.1 %forecast_and_reduce.1 = (f32[4,3,16,16,256]{4,3,2,1,0:T(8,128)S(1)}, f32[64,128]{1,0:T(8,128)S(1)}) custom-call(s32[1,64]{1,0:T(1,128)} %bitcast.4, f32[768,256]{1,0:T(8,128)} %bitcast.3, f32[16,256]{1,0:T(8,128)} %depth.1, s32[4,64,128]{2,1,0:T(8,128)} %cells_hbm.1, f32[4,64,128]{2,1,0:T(8,128)} %weights_hbm.1, f32[1,128,2,128]{3,2,1,0:T(2,128)} %values.1, ...), custom_call_target="tpu_custom_call" | custom-call | tf_op jit(solution)/shard_map/forecast_and_reduce/pallas_call | solution.py:511
  59.1 3.7 %combine_members.1 = f32[768,256]{1,0:T(8,128)} custom-call(f32[64,128]{1,0:T(8,128)S(1)} %get-tuple-element.7.total, f32[4,3,16,16,256]{4,3,2,1,0:T(8,128)S(1)} %get-tuple-element.8.fc), custom_call_target="tpu_custom_call" | custom-call | tf_op jit(solution)/shard_map/combine_members/pallas_call | solution.py:570

commit v5 on v4

--- a/solution.py
+++ b/solution.py
@@ -110,7 +110,7 @@
 
 def main_kernel(
     owners_hbm, state, depth, cells_hbm, weights_hbm, values, precisions, fc, total,
-    owners, st, dp, cells, weights, S, DB, H1, U1, V1, H2, packed, inverse, pred, XH, XL, sent, tab, picked, given, Gs, rs, zs, zb, ga,
+    owners, st, dp, dp_edge, cells, weights, S, DB, H1, U1, V1, H2, packed, inverse, pred, XH, XL, sent, tab, picked, given, Gs, rs, zs, zb, ga,
     load_sem, halo_send, halo_recv, ag_send, ag_recv, tab_send, tab_recv, red_send, red_recv, round_sem, pick_send, pick_recv,
 ):
     s = lax.axis_index("space")
@@ -199,7 +199,7 @@
     halos = []
     for n, (peer, src, dst) in enumerate(((left, HALO, HALO + ROWS), (right, ROWS, 0))):
         for k, (buf, lead, skip, rows) in enumerate(
-            ((S, (EAST,), 0, HALO), (S, (pl.ds(HEIGHT, 2),), n, HALO - 1), (DB, (), 0, HALO))
+            ((S, (EAST,), 0, HALO), (S, (pl.ds(HEIGHT, 2),), n, HALO - 1))
         ):
             halos.append(
                 pltpu.make_async_remote_copy(
@@ -209,6 +209,15 @@
             )
             halos[-1].start()
 
+    for n, (peer, src) in enumerate(((left, 0), (right, 8))):
+        halos.append(
+            pltpu.make_async_remote_copy(
+                src_ref=dp.at[pl.ds(src, 8)], dst_ref=dp_edge.at[1 - n], send_sem=halo_send.at[n, 2], recv_sem=halo_recv.at[n, 2],
+                device_id=(peer, y), device_id_type=MESH,
+            )
+        )
+        halos[-1].start()
+
     tell(0)
 
     @pl.loop(HALO + 1, HALO + ROWS - 1, unroll=2)
@@ -232,8 +241,8 @@
     inside_low = jnp.where(s > 0, 1.0, 0.0).astype(jnp.float32)
     inside_high = jnp.where(s < NS - 1, 1.0, 0.0).astype(jnp.float32)
     for i in range(HALO):
-        DB[i] = DB[i] * inside_low
-        DB[HALO + ROWS + i] = DB[HALO + ROWS + i] * inside_high
+        DB[i] = jnp.broadcast_to(dp_edge[0, pl.ds(8 - HALO + i, 1), :], (8, COLS)) * inside_low
+        DB[HALO + ROWS + i] = jnp.broadcast_to(dp_edge[1, pl.ds(i, 1), :], (8, COLS)) * inside_high
     for i in range(1, 5):
         height_step(i, inside_low if i < HALO else 1.0, S, DB, H1)
         height_step(EXT - 1 - i, inside_high if i < HALO else 1.0, S, DB, H1)
@@ -298,14 +307,23 @@
     own_row = pltpu.make_async_copy(row_for(s), tab.at[s], load_sem.at[8])
     own_row.start()
 
-    @pl.loop(1, NS)
-    def _(i):
-        peer = s + i
-        peer = peer - jnp.where(peer >= NS, NS, 0)
+    columns = [((x + dx) % 4) * (2 * NZ) + nc for dx in (2, 1, 3, 0) for nc in (1 - core, core)]
+
+    def send_row(peer):
         pltpu.make_async_remote_copy(
             src_ref=row_for(peer), dst_ref=tab.at[s], send_sem=tab_send, recv_sem=tab_recv,
             device_id=(peer, y), device_id_type=MESH,
         ).start()
+
+    @pl.loop(0, NZ - 1)
+    def _(k):
+        step = (k + 1) // 2
+        there = (z + NZ // 2 + jnp.where(k % 2 == 1, step, NZ - step)) % NZ
+        for column in columns:
+            send_row(column + there * 2)
+
+    for column in columns[:-1]:
+        send_row(column + z * 2)
 
     up_last.wait_recv()
     down_last.wait_recv()
@@ -320,7 +338,7 @@
     pack_block(y_far, lambda r: fc[y_far, 0, r], packed, inverse)
     rest = [y_low, y_high, y_far]
     interpolate(0, (0, BLK), rest, packed, inverse, cells, weights, pred)
-    interpolate(1, (0, BLK // 2), rest, packed, inverse, cells, weights, pred)
+    interpolate(1, (0, BLK // 4), rest, packed, inverse, cells, weights, pred)
 
     loads[5].wait()
     blocks = 8192 // NS
@@ -358,7 +376,7 @@
     given[y] = picked[y]
     up_v = share(fc.at[y, 2], fc.at[y, 2], 10, y_high)
     down_v = share(fc.at[y, 2], fc.at[y, 2], 11, y_low)
-    interpolate(1, (BLK // 2, BLK), rest, packed, inverse, cells, weights, pred)
+    interpolate(1, (BLK // 4, BLK), rest, packed, inverse, cells, weights, pred)
     hear(7)
     for copy in hand:
         copy.wait_recv()
@@ -488,6 +506,7 @@
     mixing = coef + (1.0 - jnp.sum(coef, axis=1, keepdims=True)) * (1.0 / M)
     mix_high, mix_low = two_terms(mixing)
     mix = jnp.concatenate([mix_high, mix_high, mix_low], axis=1)
+    stores = []
     for f in range(3):
 
         @pl.loop(0, ROWS, unroll=ROWS)
@@ -496,11 +515,12 @@
             prior = jnp.concatenate([high, low, high], axis=0)
             new = jnp.dot(mix, prior, preferred_element_type=jnp.float32)
             for c in range(2):
-                held[c, pl.ds(f * ROWS + r, LM, stride=3 * ROWS), :] = new[:, c * OBS : (c + 1) * OBS]
-
-    stores = [pltpu.make_async_copy(held.at[c], out.at[:, pl.ds(c * OBS, OBS)], sem.at[c]) for c in range(2)]
-    for store in stores:
-        store.start()
+                held[2 * f + c, pl.ds(r, LM, stride=ROWS), :] = new[:, c * OBS : (c + 1) * OBS]
+
+        for c in range(2):
+            ready = held.at[2 * f + c].reshape(LM, ROWS, OBS)
+            stores.append(pltpu.make_async_copy(ready, out.at[:, f, :, pl.ds(c * OBS, OBS)], sem.at[2 * f + c]))
+            stores[-1].start()
     for store in stores:
         store.wait()
 
@@ -521,6 +541,7 @@
             pltpu.VMEM((1, 8192 // NS), jnp.int32),
             pltpu.VMEM((2, LM * 3 * ROWS, OBS), f32),
             pltpu.VMEM((ROWS, COLS), f32),
+            pltpu.VMEM((2, 8, COLS), f32),
             pltpu.VMEM((4, BLK, OBS), jnp.int32),
             pltpu.VMEM((4, BLK, OBS), f32),
             pltpu.VMEM((3, EXT, LM, COLS), f32),
@@ -570,17 +591,17 @@
     out = pl.pallas_call(
         combine_kernel,
         name="combine_members",
-        out_shape=jax.ShapeDtypeStruct((LM * 3 * ROWS, COLS), f32),
+        out_shape=jax.ShapeDtypeStruct((LM, 3, ROWS, COLS), f32),
         in_specs=[vmem, vmem],
         out_specs=any_space,
         scratch_shapes=[
             pltpu.VMEM((M, 2 * M), f32),
-            pltpu.VMEM((2, LM * 3 * ROWS, OBS), f32),
-            pltpu.SemaphoreType.DMA((2,)),
+            pltpu.VMEM((6, LM * ROWS, OBS), f32),
+            pltpu.SemaphoreType.DMA((6,)),
         ],
         compiler_params=pltpu.CompilerParams(vmem_limit_bytes=40 << 20),
     )(total, fc)
-    return out.reshape(LM, 3, ROWS, COLS)
+    return out
 
 
 def solution(mesh):

time: 62.9 us -> 61.8 us (0.983)
  Pallas kernels: 62.8 us -> 61.7 us
    pallas_call x1, Pallas kernels: 59.1 us -> 57.9 us  [local(): pl.pallas_call(main_kernel, name='forecast_and_reduce', out_shape=(jax.Sh...]
where the time goes in v5:
time: 61.8 us; the launch traced here: 61.7 us
  Pallas kernels  61.7 us (100%)
    pallas_call x1, Pallas kernels, local(): pl.pallas_call(main_kernel, name='forecast_and_reduce', out_shape=(jax.Sh...  57.9 us
    pallas_call x1, Pallas kernels, local(): pl.pallas_call(combine_kernel, name='combine_members', out_shape=jax.Shap...  3.78 us

profile of v5, /device:TPU:1, one launch (start us, length us, event | category | flops | bytes accessed | tf_op | source)
XLA Modules:
  0.0 61.7 jit_solution(12324681472029395366)
XLA Ops:
  0.0 57.9 %forecast_and_reduce.1 = (f32[4,3,16,16,256]{4,3,2,1,0:T(8,128)S(1)}, f32[64,128]{1,0:T(8,128)S(1)}) custom-call(s32[1,64]{1,0:T(1,128)} %bitcast.3, f32[768,256]{1,0:T(8,128)} %bitcast.2, f32[16,256]{1,0:T(8,128)} %depth.1, s32[4,64,128]{2,1,0:T(8,128)} %cells_hbm.1, f32[4,64,128]{2,1,0:T(8,128)} %weights_hbm.1, f32[1,128,2,128]{3,2,1,0:T(2,128)} %values.1, ...), custom_call_target="tpu_custom_call" | custom-call | tf_op jit(solution)/shard_map/forecast_and_reduce/pallas_call | solution.py:531
  57.9 3.8 %combine_members.1 = f32[16,3,16,256]{3,2,1,0:T(8,128)} custom-call(f32[64,128]{1,0:T(8,128)S(1)} %get-tuple-element.7.total, f32[4,3,16,16,256]{4,3,2,1,0:T(8,128)S(1)} %get-tuple-element.8.fc), custom_call_target="tpu_custom_call" | custom-call | tf_op jit(solution)/shard_map/combine_members/pallas_call | solution.py:591

commit v6 on v5

--- a/solution.py
+++ b/solution.py
@@ -188,12 +188,14 @@
         terms[M : 2 * M] = jnp.zeros((M, BLK * OBS), jnp.bfloat16)
     for load in loads[:3]:
         load.wait()
-    for f in range(3):
-        for r in range(ROWS):
-            for c in range(2):
-                S[FIELD[f], HALO + r, :, c * OBS : (c + 1) * OBS] = st[c, pl.ds(f * ROWS + r, LM, stride=3 * ROWS), :]
-    for r in range(ROWS):
-        DB[HALO + r] = jnp.broadcast_to(dp[pl.ds(r, 1), :], (8, COLS))
+
+    def stage(rows):
+        for f in range(3):
+            for r in rows:
+                for c in range(2):
+                    S[FIELD[f], HALO + r, :, c * OBS : (c + 1) * OBS] = st[c, pl.ds(f * ROWS + r, LM, stride=3 * ROWS), :]
+
+    stage([*range(HALO), *range(ROWS - HALO, ROWS)])
     pl.semaphore_wait(barrier, len(near))
 
     halos = []
@@ -219,6 +221,9 @@
         halos[-1].start()
 
     tell(0)
+    stage(range(HALO, ROWS - HALO))
+    for r in range(ROWS):
+        DB[HALO + r] = jnp.broadcast_to(dp[pl.ds(r, 1), :], (8, COLS))
 
     @pl.loop(HALO + 1, HALO + ROWS - 1, unroll=2)
     def _(i):

time: 61.8 us -> 61.8 us (level)
  no operation moved by 1% of the time
where the time goes in v6:
time: 61.8 us; the launch traced here: 61.7 us
  Pallas kernels  61.7 us (100%)
    pallas_call x1, Pallas kernels, local(): pl.pallas_call(main_kernel, name='forecast_and_reduce', out_shape=(jax.Sh...  57.9 us
    pallas_call x1, Pallas kernels, local(): pl.pallas_call(combine_kernel, name='combine_members', out_shape=jax.Shap...  3.78 us

profile of v6, /device:TPU:1, one launch (start us, length us, event | category | flops | bytes accessed | tf_op | source)
XLA Modules:
  0.0 61.7 jit_solution(17852896310922700290)
XLA Ops:
  0.0 57.9 %forecast_and_reduce.1 = (f32[4,3,16,16,256]{4,3,2,1,0:T(8,128)S(1)}, f32[64,128]{1,0:T(8,128)S(1)}) custom-call(s32[1,64]{1,0:T(1,128)} %bitcast.3, f32[768,256]{1,0:T(8,128)} %bitcast.2, f32[16,256]{1,0:T(8,128)} %depth.1, s32[4,64,128]{2,1,0:T(8,128)} %cells_hbm.1, f32[4,64,128]{2,1,0:T(8,128)} %weights_hbm.1, f32[1,128,2,128]{3,2,1,0:T(2,128)} %values.1, ...), custom_call_target="tpu_custom_call" | custom-call | tf_op jit(solution)/shard_map/forecast_and_reduce/pallas_call | solution.py:536
  57.9 3.8 %combine_members.1 = f32[16,3,16,256]{3,2,1,0:T(8,128)} custom-call(f32[64,128]{1,0:T(8,128)S(1)} %get-tuple-element.7.total, f32[4,3,16,16,256]{4,3,2,1,0:T(8,128)S(1)} %get-tuple-element.8.fc), custom_call_target="tpu_custom_call" | custom-call | tf_op jit(solution)/shard_map/combine_members/pallas_call | solution.py:596
